TPU v7x, 512 devices: a whole 4x4x16 slice. The times are simulated.
512 devices in a mesh: req: 128 (over x, z, core), tp: 4 (over y).
Axes of the slice: x: 4, y: 4, z: 16, core: 2. Of those that a mesh axis runs over, the one named last changes fastest.
Arguments:
- queries: bfloat16 [2, 128, 32, 1536], P(None, 'req', None, 'tp')
- response_kv: bfloat16 [2, 128, 2, 32, 256], P(None, 'req'), may hold values from -6 to 6
- cache_kv: bfloat16 [2, 128, 2, 384, 256], P(None, 'req'), may hold values from -6 to 6
- residual: bfloat16 [2, 128, 32, 1536], P(None, 'req')
- out_proj: bfloat16 [2, 1536, 1536], P(None, 'tp'), may hold values from -0.5 to 0.5
- norm_gain: float32 [2, 1536], replicated, may hold values from 0.25 to 1.75
- lm_head: bfloat16 [2, 131072, 1536], P(None, 'req', 'tp')
- targets: int32 [128, 32], P(None, 'tp'), may hold values from 0 to 131071
- resp_lengths: int32 [128], replicated, may hold values from 1 to 32, 2560 in all
- cache_lengths: int32 [128], P('req'), may hold values from 1 to 384, 30720 in all
- owner_slot: int32 [128], replicated, may hold values from 0 to 127, each once
- sink_count: int32 [1], replicated, may hold values from 1 to 95
- window_size: int32 [1], replicated, may hold values from 48 to 191
Outputs:
- token_logprobs: float32 [128, 32], P('req', 'tp')
- request_scores: float32 [128, 2], P('req')
Inputs may be any that keep to these rules, and one draw needn't show every extreme that they name: `resp_lengths`: live response slots are the first ones; all lengths sum to 2560. `cache_lengths`: live cache slots are the first ones; all lengths sum to 30720. `owner_slot`: A permutation of the requests.
All inputs are finite; a program needn't handle non-finite values. No bound on the sum of `cache_lengths` on one device may be relied on, other than what follows from the above.
Results may differ from a plain program's by a relative error of at most 0.0014.
Values may be sent and summed in bfloat16 or wider, within the bound.
A program may use at most 128 MiB of HBM per device.

v0:
```python
import jax
import jax.numpy as jnp
from jax import lax
from jax.sharding import PartitionSpec as P

HEADS = 12
HEAD = 128
KV_HEADS = 2
RESP = 32
CACHE = 384


def span_mask(lengths, sink_count, window_size):
    cache_pos = jnp.arange(CACHE, dtype=jnp.int32)
    slot_pos = jnp.arange(RESP, dtype=jnp.int32)
    req_count = lengths.shape[0]
    key_pos = jnp.concatenate([cache_pos[None, :], lengths[:, None] + slot_pos[None, :]], axis=1)
    key_live = jnp.concatenate(
        [cache_pos[None, :] < lengths[:, None], jnp.ones((req_count, RESP), jnp.bool_)], axis=1
    )
    query_pos = lengths[:, None] + slot_pos[None, :]
    earlier = key_pos[:, None, :] <= query_pos[:, :, None]
    inside = (key_pos[:, None, :] < sink_count[0]) | (
        query_pos[:, :, None] - key_pos[:, None, :] < window_size[0]
    )
    return key_live[:, None, :] & earlier & inside


def rms_norm(hidden, norm_gain):
    scale_inv = lax.rsqrt(jnp.mean(hidden * hidden, axis=-1, keepdims=True) + 1e-06)
    return (hidden * scale_inv * norm_gain[:, None, None, :]).astype(jnp.bfloat16)


def per_device(
    queries,
    response_kv,
    cache_kv,
    residual,
    out_proj,
    norm_gain,
    lm_head,
    targets,
    resp_lengths,
    cache_lengths,
    owner_slot,
    sink_count,
    window_size,
):
    tp_size = lax.axis_size("tp")
    tp_index = lax.axis_index("tp")
    req_index = lax.axis_index("req")
    local_reqs = queries.shape[1]
    local_heads = HEADS // tp_size
    group_size = HEADS // KV_HEADS
    kv_index = tp_index * local_heads // group_size
    quarter = RESP // tp_size
    cache_head = lax.dynamic_slice_in_dim(cache_kv, kv_index * HEAD, HEAD, axis=4)
    resp_head = lax.dynamic_slice_in_dim(response_kv, kv_index * HEAD, HEAD, axis=4)
    key_rows = jnp.concatenate([cache_head[:, :, 0], resp_head[:, :, 0]], axis=2)
    value_rows = jnp.concatenate([cache_head[:, :, 1], resp_head[:, :, 1]], axis=2)
    query_heads = queries.reshape(2, local_reqs, RESP, local_heads, HEAD)
    scores = jnp.einsum(
        "mrshd,mrkd->mrhsk", query_heads, key_rows, preferred_element_type=jnp.float32
    ) * HEAD ** (-0.5)
    allowed = span_mask(cache_lengths, sink_count, window_size)[None, :, None]
    masked = jnp.where(allowed, scores, -jnp.inf)
    row_peak = jnp.max(masked, axis=-1, keepdims=True)
    weights = jnp.exp(masked - row_peak)
    weights = (weights / jnp.sum(weights, axis=-1, keepdims=True)).astype(jnp.bfloat16)
    attended = jnp.einsum(
        "mrhsk,mrkd->mrshd", weights, value_rows, preferred_element_type=jnp.float32
    )
    attended = attended.astype(jnp.bfloat16).reshape(2, local_reqs, RESP, local_heads * HEAD)
    partial_value = jnp.einsum(
        "mrsf,mfd->mrsd", attended, out_proj, preferred_element_type=jnp.float32
    )
    start_slot = tp_index * quarter
    projected = lax.dynamic_slice_in_dim(lax.psum(partial_value, "tp"), start_slot, quarter, axis=2)
    own_residual = lax.dynamic_slice_in_dim(residual, start_slot, quarter, axis=2)
    hidden = own_residual.astype(jnp.float32) + projected
    normed = rms_norm(hidden, norm_gain)
    flat_rows = normed.reshape(2, local_reqs * quarter, normed.shape[3])
    full_head = lax.all_gather(lm_head, "tp", axis=2, tiled=True)
    vocab_rows = full_head.shape[1]
    vocab_start = req_index * vocab_rows
    flat_targets = targets.reshape(-1)
    total_rows = flat_targets.shape[0]
    requests = total_rows // quarter
    logits = jnp.einsum(
        "mnd,mvd->mnv",
        lax.all_gather(flat_rows, "req", axis=1, tiled=True),
        full_head,
        preferred_element_type=jnp.float32,
    )
    block_peak = jnp.max(logits, axis=-1)
    block_total = jnp.sum(jnp.exp(logits - block_peak[..., None]), axis=-1)
    wanted = flat_targets - vocab_start
    target_hits = jnp.arange(vocab_rows, dtype=jnp.int32)[None, None, :] == wanted[None, :, None]
    block_pick = jnp.sum(jnp.where(target_hits, logits, 0.0), axis=-1)
    peak_all = block_peak
    total_all = block_total
    picked_all = block_pick
    peak_all = peak_all.reshape(2, requests, quarter)
    total_all = total_all.reshape(2, requests, quarter)
    picked_all = picked_all.reshape(2, requests, quarter)
    row_order = (
        jnp.zeros((requests,), jnp.int32).at[owner_slot].set(jnp.arange(requests, dtype=jnp.int32))
    )
    owned_reqs = lax.dynamic_slice_in_dim(row_order, req_index * local_reqs, local_reqs)
    vocab_top = lax.pmax(peak_all, "req")
    exp_total, picked = lax.psum((total_all * jnp.exp(peak_all - vocab_top), picked_all), "req")
    logprob = (picked - (vocab_top + jnp.log(exp_total)))[:, owned_reqs]
    lengths_owned = resp_lengths[owned_reqs]
    live_slots = (start_slot + jnp.arange(quarter, dtype=jnp.int32))[None, :] < lengths_owned[
        :, None
    ]
    policy = jnp.where(live_slots, logprob[0], 0.0)
    log_ratio = jnp.where(live_slots, logprob[0] - logprob[1], 0.0)
    policy_total, ratio_total = lax.psum(
        (jnp.sum(policy, axis=1), jnp.sum(log_ratio, axis=1)), "tp"
    )
    counts = lengths_owned.astype(jnp.float32)
    request_scores = jnp.stack([policy_total / counts, ratio_total / counts], axis=1)
    return (policy, request_scores)


def solution(mesh):
    in_specs = (
        P(None, "req", None, "tp"),
        P(None, "req", None, None, None),
        P(None, "req", None, None, None),
        P(None, "req", None, None),
        P(None, "tp", None),
        P(),
        P(None, "req", "tp"),
        P(None, "tp"),
        P(),
        P("req"),
        P(),
        P(),
        P(),
    )
    out_specs = (P("req", "tp"), P("req", None))
    return jax.shard_map(
        per_device, mesh=mesh, in_specs=in_specs, out_specs=out_specs, check_vma=False
    )
```

profile of v0, /device:TPU:1, one launch (start us, length us, event | category | flops | bytes accessed | tf_op | source)
XLA Modules:
  0.0 1321.6 jit_solution(16412632593061100903)
XLA Ops:
  7.2 0.0 copy-start
  7.2 0.0 copy-start.1
  7.2 0.0 copy-start.2
  7.2 0.0 copy-start.3
  7.2 0.0 copy-start.4
  7.2 0.0 copy-start.5
  7.2 0.0 all-reduce.5.cloned.1.call-start
  7.3 1.2 dynamic-slice_bitcast_fusion
  8.5 0.8 dynamic-slice_bitcast_fusion.2
  11.3 0.8 reshape.303
  12.1 0.1 fusion.12
  12.2 0.3 fusion.23
  12.5 0.2 fusion.5
  12.8 0.3 fusion.4
  13.1 0.1 reshape.305
  13.1 0.0 copy-done
  13.2 1.3 convolution_bitcast_fusion
  14.4 0.0 all-reduce.5.cloned.1.call-update
  14.5 0.0 all-gather.4.cloned.1.call-start
  14.5 0.7 all-gather.4.cloned.1.call-update
  15.2 0.0 all-gather.6.cloned.1.call-start
  15.3 60.2 %all-reduce.5.cloned.1.call-done = f32[2,1,32,1536]{3,2,0,1:T(8,128)} async-done(((f32[2,1,32,1536]{3,2,0,1:T(8,128)}), f32[2,1,32,1536]{3,2,0,1:T(8,128)}) %all-reduce.5.cloned.1.call-update) | async-done | bytes 393232 | tf_op jit(solution)/shard_map/psum | solution.py:78
  75.5 0.0 copy-done.1
  75.5 1.0 multiply_reduce_fusion
  76.5 0.0 copy-done.2
  76.5 1.6 multiply_convert_fusion
  78.1 0.0 all-gather.6.cloned.1.call-update
  78.1 0.0 copy-done.3
  78.1 0.1 copy.19
  78.2 0.1 sub.65
  78.3 0.0 copy-done.4
  78.3 1.0 scatter_custom_fusion
  79.3 0.6 dynamic_slice.15
  81.9 0.0 copy-done.5
  81.9 0.6 dynamic-slice.5
  83.1 0.8 iota_compare_fusion
  83.9 70.0 %all-gather.4.cloned.1.call-done = bf16[2,1024,1536]{2,1,0:T(8,128)(2,1)} async-done(((bf16[2,1024,384]{2,1,0:T(8,128)(2,1)}), bf16[2,1024,1536]{2,1,0:T(8,128)(2,1)}) %all-gather.4.cloned.1.call-update) | async-done | bytes 6291472 | tf_op jit(solution)/shard_map/all_gather | solution.py:83
  153.9 149.6 %all-gather.6.cloned.1.call-done = bf16[2,1,1024,1536]{3,2,0,1:T(8,128)(2,1)} async-done(((bf16[2,1,8,1536]{3,2,0,1:T(8,128)(2,1)}), bf16[2,1,1024,1536]{3,2,0,1:T(8,128)(2,1)}) %all-gather.6.cloned.1.call-update) | async-done | bytes 6291472 | tf_op jit(solution)/shard_map/all_gather | solution.py:91
  303.5 12.7 fusion.24
  316.2 0.1 reshape.308
  316.3 5.1 exponential_reduce_fusion
  321.4 0.8 reshape.309
  322.2 487.8 %pmax.7 = f32[2,128,8]{2,1,0:T(8,128)S(1)} all-reduce(f32[2,128,8]{2,1,0:T(8,128)S(1)} %reshape.308), channel_id=1, replica_groups=mesh['req'=128,'tp'=4] {'req'}, use_global_device_ids=true, to_apply=%region_8.9 | all-reduce | flops 2048 | bytes 16384 | tf_op jit(solution)/shard_map/pmax | solution.py:110
  810.0 0.1 reshape.307
  810.2 490.9 %all-reduce.1 = (f32[2,128,8]{2,1,0:T(8,128)S(1)}, f32[2,128,8]{2,1,0:T(8,128)S(1)}) all-reduce(f32[2,128,8]{2,1,0:T(8,128)S(1)} %reshape.307, f32[2,128,8]{2,1,0:T(8,128)S(1)} %exponential_multiply_fusion), channel_id=1, replica_groups=mesh['req'=128,'tp'=4] {'req'}, use_global_device_ids=true, to_apply=%region_6.7 | all-reduce | flops 4096 | bytes 32768 | tf_op jit(solution)/shard_map/psum | solution.py:111
  1301.1 1.2 fusion.17
  1302.3 1.7 fusion.22
  1304.0 9.1 all-reduce.2
  1314.5 0.6 pad_maximum_fusion
  (14 shorter events, 0.2 us)
Async XLA Ops:
  7.2 6.0 copy-start
  7.2 68.3 %copy-start.1 = (bf16[2,1,32,1536]{3,2,1,0:T(8,128)(2,1)S(1)}, bf16[2,1,32,1536]{3,2,1,0:T(8,128)(2,1)}, u32[]{:S(2)}) copy-start(bf16[2,1,32,1536]{3,2,1,0:T(8,128)(2,1)} %param.16) | copy-start | bytes 589828
  7.2 69.3 %copy-start.2 = (f32[2,1536]{1,0:T(2,128)S(1)}, f32[2,1536]{1,0:T(2,128)}, u32[]{:S(2)}) copy-start(f32[2,1536]{1,0:T(2,128)} %param.18) | copy-start | bytes 36868
  7.2 70.9 %copy-start.3 = (s32[128,8]{0,1:T(8,128)S(1)}, s32[128,8]{0,1:T(8,128)}, u32[]{:S(2)}) copy-start(s32[128,8]{0,1:T(8,128)} %param.20) | copy-start | bytes 12292
  7.2 71.1 %copy-start.4 = (s32[128]{0:T(128)S(1)}, s32[128]{0:T(128)}, u32[]{:S(2)}) copy-start(s32[128]{0:T(128)} %param.23) | copy-start | bytes 1540
  7.2 74.6 %copy-start.5 = (s32[128]{0:T(128)S(1)}, s32[128]{0:T(128)}, u32[]{:S(2)}) copy-start(s32[128]{0:T(128)} %param.21) | copy-start | bytes 1540
  7.2 68.2 %all-reduce.5.cloned.1.call-start = ((), (), s32[]{:S(2)}) async-start(), calls=%async_computation | async-start | bytes 786432 | tf_op jit(solution)/shard_map/psum | solution.py:78
  14.5 139.5 %all-gather.4.cloned.1.call-start = ((), (), s32[]{:S(2)}) async-start(), calls=%async_computation.1 | async-start | bytes 7864320 | tf_op jit(solution)/shard_map/all_gather | solution.py:83
  15.2 288.3 %all-gather.6.cloned.1.call-start = ((), (), s32[]{:S(2)}) async-start(), calls=%async_computation.2 | async-start | bytes 6340608 | tf_op jit(solution)/shard_map/all_gather | solution.py:91
Sparse Core Ops, SparseCore 0:
  14.6 60.8 all-reduce.4
  77.8 76.0 all-gather.3
  157.6 145.8 all-gather.5
where the time goes:
time: 1330 us; the launch traced here: 1320 us
  blocking collectives  988 us (74%)
  waiting for transfers between devices  281 us (21%)
  between operations  19.9 us (1%)
  matrix products  14.6 us (1%)
    psum x1, blocking collectives, per_device(): lax.psum((total_all * jnp.exp(peak_all - vocab_top), picked_all), 'req')  491 us
    pmax x1, blocking collectives, per_device(): vocab_top = lax.pmax(peak_all, 'req')  488 us
    all_gather x1, waiting for transfers between devices, per_device(): lax.all_gather(flat_rows, 'req', axis=1, tiled=True)  150 us
    all_gather x1, waiting for transfers between devices, per_device(): full_head = lax.all_gather(lm_head, 'tp', axis=2, tiled=True)  70 us
    psum x1, waiting for transfers between devices, per_device(): lax.psum(partial_value, 'tp')  60.2 us
  transfers between devices with their start and end apart: 3, of which 3 were waited for; matrix products, arithmetic and copies ran while one was open for 0% of the time, Pallas kernels for 0%

commit v1 on v0

v1 whole, which is shorter than its diff:
```python
import jax
import jax.numpy as jnp
from jax import lax
from jax.experimental import pallas as pl
from jax.experimental.pallas import tpu as pltpu
from jax.sharding import PartitionSpec as P

HEADS = 12
HEAD = 128
KV_HEADS = 2
RESP = 32
CACHE = 384
D = 1536

NX, NZ, NC, NT = 4, 16, 2, 4
REQS = NX * NZ * NC
SLOTS = 16
FEAT = D // NT
VOCAB_BLOCK = 1024
PIECES = 4
PIECE = VOCAB_BLOCK // PIECES
MESH = pl.DeviceIdType.MESH
EXACT = lax.Precision.HIGHEST


def span_mask(lengths, sink_count, window_size):
    cache_pos = jnp.arange(CACHE, dtype=jnp.int32)
    slot_pos = jnp.arange(RESP, dtype=jnp.int32)
    req_count = lengths.shape[0]
    key_pos = jnp.concatenate([cache_pos[None, :], lengths[:, None] + slot_pos[None, :]], axis=1)
    key_live = jnp.concatenate(
        [cache_pos[None, :] < lengths[:, None], jnp.ones((req_count, RESP), jnp.bool_)], axis=1
    )
    query_pos = lengths[:, None] + slot_pos[None, :]
    earlier = key_pos[:, None, :] <= query_pos[:, :, None]
    inside = (key_pos[:, None, :] < sink_count[0]) | (
        query_pos[:, :, None] - key_pos[:, None, :] < window_size[0]
    )
    return key_live[:, None, :] & earlier & inside


def iota(shape, dim):
    return lax.broadcasted_iota(jnp.int32, shape, dim)


def nt_dot(a, b, precision=None):
    return lax.dot_general(
        a, b, (((1,), (1,)), ((), ())), precision=precision, preferred_element_type=jnp.float32
    )


def fused(
    partial, residual, gain, head, targets, lengths, owner,
    policy_out, scores_out,
    hbuf, rows, rs_in, tgt_in, tgt_all, own_all, xbuf, outbuf, in1, ex2, in2, lpbuf, in3,
    local_sem, rs_s, rs_r, tg_s, tg_r, hp_s, hp_r, hq_s, hq_r, hf_s, hf_r,
    x_s, x_r, zr_s, zr_r, zl_s, zl_r, cr_s, cr_r, cl_s, cl_r, e1_s, e1_r, e2_s, e2_r, e3_s, e3_r,
):
    req = lax.axis_index("req")
    t = lax.axis_index("tp")
    x = req // (NZ * NC)
    z = (req // NC) % NZ
    c = req % NC
    model = t // 2
    half = t % 2
    pair = t + 1 - 2 * (t % 2)
    across = NT - 1 - t

    def index_of(px, pz, pc):
        return (px * NZ + pz) * NC + pc

    def send(src, dst, ssem, rsem, preq, pt):
        return pltpu.make_async_remote_copy(
            src_ref=src, dst_ref=dst, send_sem=ssem, recv_sem=rsem,
            device_id={"req": preq, "tp": pt}, device_id_type=MESH,
        )

    barrier = pltpu.get_barrier_semaphore()

    def greet(preq, pt):
        pl.semaphore_signal(
            barrier, inc=1, device_id={"req": preq, "tp": pt}, device_id_type=MESH
        )

    for d in range(1, NT):
        greet(req, (t + d) % NT)
    group = x * NC + c
    for d in range(1, NX * NC):
        other = (group + d) % (NX * NC)
        greet(index_of(other // NC, z, other % NC), t)
    for d in range(1, NZ):
        greet(index_of(x, (z + d) % NZ, c), t)
    pl.semaphore_wait(barrier, (NT - 1) + (NX * NC - 1) + (NZ - 1))

    def rs_copy(d):
        pt = (t + d) % NT
        start = pl.multiple_of((pt % 2) * SLOTS, SLOTS)
        return send(
            partial.at[pt // 2, pl.ds(start, SLOTS)], rs_in.at[d], rs_s.at[d], rs_r.at[d], req, pt
        )

    for d in range(1, NT):
        rs_copy(d).start()

    def lanes(source):
        return pl.ds(pl.multiple_of(source * FEAT, FEAT), FEAT)

    def piece(k):
        return pl.ds(k * PIECE, PIECE)

    def pair_copy(k):
        return send(
            head.at[model, piece(k)], hbuf.at[piece(k), lanes(t)], hp_s.at[k], hp_r.at[k], req, pair
        )

    def across_copy(k):
        return send(
            head.at[1 - model, piece(k)], hbuf.at[piece(k), lanes(t)], hq_s.at[k], hq_r.at[k],
            req, across,
        )

    def across_recv(k):
        return send(
            head.at[1 - model, piece(k)], hbuf.at[piece(k), lanes(across)], hq_s.at[k], hq_r.at[k],
            req, across,
        )

    def forward_copy(k):
        part = hbuf.at[piece(k), lanes(across)]
        return send(part, part, hf_s.at[k], hf_r.at[k], req, pair)

    def pair_recv(k):
        part = hbuf.at[piece(k), lanes(pair)]
        return send(part, part, hp_s.at[k], hp_r.at[k], req, pair)

    def forward_recv(k):
        part = hbuf.at[piece(k), lanes(NT - 1 - pair)]
        return send(part, part, hf_s.at[k], hf_r.at[k], req, pair)

    for k in range(PIECES):
        across_copy(k).start()
        pair_copy(k).start()
    own_head = pltpu.make_async_copy(head.at[model], hbuf.at[:, lanes(t)], local_sem)
    own_head.start()

    req_sub = iota((REQS, 128), 0)
    lane_l = iota((REQS, 128), 1)
    same_xc = ((req_sub >> 5) == (lane_l >> 5)) & ((req_sub & 1) == ((lane_l >> 4) & 1))
    same_z = ((iota((NZ, REQS), 1) >> 1) & (NZ - 1)) == iota((NZ, REQS), 0)
    zmask = jnp.where(same_z, 1.0, 0.0)
    spread = jnp.where(
        (iota((8, 128), 1) & (SLOTS - 1)) == iota((8, 128), 0) + 8 * half, 1.0, 0.0
    )
    wide = jnp.dot(
        targets[...].astype(jnp.float32), spread, precision=EXACT,
        preferred_element_type=jnp.float32,
    )
    placed = jnp.dot(
        zmask, jnp.where(same_xc, wide, 0.0), precision=EXACT, preferred_element_type=jnp.float32
    )
    tgt_in[0] = placed.astype(jnp.int32)

    def tgt_copy(d):
        return send(tgt_in.at[0], tgt_in.at[d], tg_s.at[d], tg_r.at[d], req, (t + d) % NT)

    for d in range(1, NT):
        tgt_copy(d).start()
    own_all[...] = jnp.dot(
        zmask * owner[...].astype(jnp.float32), jnp.where(same_xc, 1.0, 0.0), precision=EXACT,
        preferred_element_type=jnp.float32,
    ).astype(jnp.int32)
    outbuf[...] = jnp.zeros_like(outbuf)

    start = pl.multiple_of(half * SLOTS, SLOTS)
    hidden = residual[model, pl.ds(start, SLOTS), :].astype(jnp.float32)
    total = partial[model, pl.ds(start, SLOTS), :]
    for d in range(1, NT):
        rs_copy(d).wait_recv()
        total = total + rs_in[d]
    hidden = hidden + total
    scale_inv = lax.rsqrt(jnp.mean(hidden * hidden, axis=-1, keepdims=True) + 1e-06)
    rows[x, z, c] = (hidden * scale_inv * gain[pl.ds(model, 1), :]).astype(jnp.bfloat16)

    def x_copy(d):
        part = rows.at[x, z, c]
        return send(part, part, x_s.at[d], x_r.at[d], index_of((x + d) % NX, z, c), t)

    def x_recv(d):
        part = rows.at[(x + NX - d) % NX, z, c]
        return send(part, part, x_s.at[d], x_r.at[d], index_of((x + NX - d) % NX, z, c), t)

    for d in range(1, NX):
        x_copy(d).start()
    for d in range(1, NX):
        x_recv(d).wait_recv()

    right = index_of(x, (z + 1) % NZ, c)
    left = index_of(x, (z + NZ - 1) % NZ, c)
    twin = index_of(x, z, 1 - c)

    def right_copy(s):
        part = rows.at[:, (z + NZ - s) % NZ, c]
        return send(part, part, zr_s.at[s], zr_r.at[s], right, t)

    def right_recv(s):
        part = rows.at[:, (z + NZ - s - 1) % NZ, c]
        return send(part, part, zr_s.at[s], zr_r.at[s], right, t)

    def left_copy(s):
        part = rows.at[:, (z + s) % NZ, c]
        return send(part, part, zl_s.at[s], zl_r.at[s], left, t)

    def left_recv(s):
        part = rows.at[:, (z + s + 1) % NZ, c]
        return send(part, part, zl_s.at[s], zl_r.at[s], left, t)

    def twin_right(s):
        part = rows.at[:, (z + NZ - s) % NZ, c]
        return send(part, part, cr_s.at[s], cr_r.at[s], twin, t)

    def twin_left(s):
        part = rows.at[:, (z + s % 8) % NZ, c]
        return send(part, part, cl_s.at[s], cl_r.at[s], twin, t)

    def twin_right_recv(s):
        part = rows.at[:, (z + NZ - s) % NZ, 1 - c]
        return send(part, part, cr_s.at[s], cr_r.at[s], twin, t)

    def twin_left_recv(s):
        part = rows.at[:, (z + s % 8) % NZ, 1 - c]
        return send(part, part, cl_s.at[s], cl_r.at[s], twin, t)

    right_copy(0).start()
    left_copy(0).start()
    twin_left(8).start()

    tgt_own = jnp.zeros((NZ, 128), jnp.int32)
    for d in range(NT):
        if d:
            tgt_copy(d).wait_recv()
        wanted_half = ((t + NT - d) % NT) // 2 == half
        tgt_own = tgt_own + jnp.where(wanted_half, tgt_in[d], 0)
    tgt_all[...] = tgt_own - req * VOCAB_BLOCK

    def ring_step(s):
        right_recv(s - 1).wait_recv()
        right_copy(s).start()
        twin_right(s).start()
        left_recv(s - 1).wait_recv()

        @pl.when(s < 7)
        def _():
            left_copy(s).start()

        twin_left(s).start()

    def first_steps(s, carry):
        ring_step(s)
        across_recv(s - 1).wait_recv()
        forward_copy(s - 1).start()
        return carry

    lax.fori_loop(1, 5, first_steps, 0)

    own_head.wait()

    def head_wait(k, carry):
        pair_recv(k).wait_recv()
        forward_recv(k).wait_recv()
        return carry

    lax.fori_loop(0, PIECES, head_wait, 0)

    def block_rows(pz):
        return rows[:, pz].reshape(NX * NC * SLOTS, D)

    def compute(k):
        z1 = (z + NZ - k) % NZ
        z2 = (z + k % 8) % NZ
        twin_right_recv(k).wait_recv()
        twin_left_recv(k).wait_recv()
        xbuf[0:128] = block_rows(z1)
        xbuf[128:256] = block_rows(z2)
        logits = nt_dot(hbuf[...], xbuf[...])
        peak = jnp.max(logits, axis=0, keepdims=True)
        norm = jnp.sum(jnp.exp(logits - peak), axis=0, keepdims=True)
        lse = peak + jnp.log(norm)
        wanted = jnp.concatenate([tgt_all[pl.ds(z1, 1), :], tgt_all[pl.ds(z2, 1), :]], axis=1)
        hit = iota((VOCAB_BLOCK, 256), 0) == wanted
        pick = jnp.sum(jnp.where(hit, logits, 0.0), axis=0, keepdims=True)
        sub = iota((128, 128), 0)
        slot = iota((128, 128), 1) & (SLOTS - 1)
        dest = ((sub >> 5) * NZ + (sub & (NZ - 1))) * NC + ((sub >> 4) & 1)
        found = jnp.zeros((128, 128), jnp.float32)
        for i, pz in enumerate((z1, z2)):
            cols = slice(128 * i, 128 * i + 128)
            values = jnp.where(
                sub == slot, lse[:, cols], jnp.where(sub == slot + SLOTS, pick[:, cols], 0.0)
            )
            select = jnp.where(dest == own_all[pl.ds(pz, 1), :], 1.0, 0.0)
            found = found + nt_dot(select, values, EXACT)
        outbuf[...] += found

    def late_steps(s, carry):
        ring_step(s)
        compute(2 * s - 9)
        compute(2 * s - 8)
        return carry

    lax.fori_loop(5, 8, late_steps, 0)
    right_recv(7).wait_recv()
    twin_right(8).start()

    def last_chunks(k, carry):
        compute(k)
        return carry

    lax.fori_loop(7, 9, last_chunks, 0)

    def e1_copy(d):
        other = (group + d) % (NX * NC)
        return send(
            outbuf.at[pl.ds(pl.multiple_of(other * NZ, NZ), NZ)], in1.at[d], e1_s.at[d], e1_r.at[d],
            index_of(other // NC, z, other % NC), t,
        )

    for d in range(1, NX * NC):
        e1_copy(d).start()
    in1[0] = outbuf[pl.ds(pl.multiple_of(group * NZ, NZ), NZ), :]
    for d in range(1, NX * NC):
        e1_copy(d).wait_recv()

    def combine(values):
        peak = jnp.max(values, axis=0, keepdims=True)
        lse = peak + jnp.log(jnp.sum(jnp.exp(values - peak), axis=0, keepdims=True))
        pick = jnp.sum(values, axis=0, keepdims=True)
        return jnp.where(iota(lse.shape, 2) < SLOTS, lse, pick)[0]

    merged = combine(in1[...])
    for k in range(NZ):
        ex2[k] = merged[k : k + 1]

    def e2_copy(d):
        pz = (z + d) % NZ
        return send(ex2.at[pz], in2.at[d], e2_s.at[d], e2_r.at[d], index_of(x, pz, c), t)

    for d in range(1, NZ):
        e2_copy(d).start()
    in2[0] = ex2[z]
    for d in range(1, NZ):
        e2_copy(d).wait_recv()
    final = combine(in2[...])
    logprob = pltpu.roll(final, 128 - SLOTS, 1) - final
    lpbuf[...] = logprob
    in3[t] = logprob

    def e3_copy(d):
        return send(lpbuf, in3.at[t], e3_s.at[d], e3_r.at[d], req, (t + d) % NT)

    def e3_recv(d):
        return send(lpbuf, in3.at[(t + NT - d) % NT], e3_s.at[d], e3_r.at[d], req, (t + d) % NT)

    for d in range(1, NT):
        e3_copy(d).start()
    count = jnp.sum(jnp.where(owner[...] == req, lengths[...], 0), axis=1, keepdims=True)
    for d in range(1, NT):
        e3_recv(d).wait_recv()
    lane = iota((1, 128), 1)
    live0 = (lane < SLOTS) & (lane < count)
    live1 = (lane < SLOTS) & (lane + SLOTS < count)
    low, high = in3[0], in3[1]
    policy_total = jnp.sum(
        jnp.where(live0, low, 0.0) + jnp.where(live1, high, 0.0), axis=1, keepdims=True
    )
    ratio_total = jnp.sum(
        jnp.where(live0, low - in3[2], 0.0) + jnp.where(live1, high - in3[3], 0.0),
        axis=1, keepdims=True,
    )
    counts = count.astype(jnp.float32)
    scores = jnp.where(lane == 0, policy_total / counts, ratio_total / counts)
    scores_out[...] = scores[:, 0:2]
    mine = in3[t // 2]
    mine = jnp.where(half == 1, pltpu.roll(mine, 120, 1), mine)
    mine = jnp.where(lane + 8 * t < count, mine, 0.0)
    policy_out[...] = mine[:, 0:8]

    for d in range(1, NT):
        rs_copy(d).wait_send()
        tgt_copy(d).wait_send()
        x_copy(d).wait_send()
        e3_copy(d).wait_send()

    def head_sent(k, carry):
        pair_copy(k).wait_send()
        across_copy(k).wait_send()
        forward_copy(k).wait_send()
        return carry

    lax.fori_loop(0, PIECES, head_sent, 0)

    def right_sent(s, carry):
        right_copy(s).wait_send()
        twin_right(s + 1).wait_send()
        twin_left(s + 1).wait_send()
        return carry

    lax.fori_loop(0, 8, right_sent, 0)

    def left_sent(s, carry):
        left_copy(s).wait_send()
        return carry

    lax.fori_loop(0, 7, left_sent, 0)
    for d in range(1, NX * NC):
        e1_copy(d).wait_send()
    for d in range(1, NZ):
        e2_copy(d).wait_send()


def fused_call(partial, residual, gain, head, targets, lengths, owner):
    dma = pltpu.SemaphoreType.DMA
    vmem = pl.BlockSpec(memory_space=pltpu.VMEM)
    counts = [NT] * 4 + [PIECES] * 6 + [NX] * 2 + [8] * 4 + [9] * 4 + [8] * 2 + [NZ] * 2 + [NT] * 2
    return pl.pallas_call(
        fused,
        out_shape=(
            jax.ShapeDtypeStruct((1, 8), jnp.float32),
            jax.ShapeDtypeStruct((1, 2), jnp.float32),
        ),
        in_specs=[vmem, vmem, vmem, pl.BlockSpec(memory_space=pl.ANY), vmem, vmem, vmem],
        out_specs=(vmem, vmem),
        scratch_shapes=[
            pltpu.VMEM((VOCAB_BLOCK, D), jnp.bfloat16),
            pltpu.VMEM((NX, NZ, NC, SLOTS, D), jnp.bfloat16),
            pltpu.VMEM((NT, SLOTS, D), jnp.float32),
            pltpu.VMEM((NT, NZ, 128), jnp.int32),
            pltpu.VMEM((NZ, 128), jnp.int32),
            pltpu.VMEM((NZ, 128), jnp.int32),
            pltpu.VMEM((256, D), jnp.bfloat16),
            pltpu.VMEM((REQS, 128), jnp.float32),
            pltpu.VMEM((NX * NC, NZ, 128), jnp.float32),
            pltpu.VMEM((NZ, 1, 128), jnp.float32),
            pltpu.VMEM((NZ, 1, 128), jnp.float32),
            pltpu.VMEM((1, 128), jnp.float32),
            pltpu.VMEM((NT, 1, 128), jnp.float32),
            dma,
        ]
        + [dma((n,)) for n in counts],
        compiler_params=pltpu.CompilerParams(
            collective_id=0, has_side_effects=True, vmem_limit_bytes=40 << 20
        ),
    )(partial, residual, gain, head, targets, lengths, owner)


def per_device(
    queries,
    response_kv,
    cache_kv,
    residual,
    out_proj,
    norm_gain,
    lm_head,
    targets,
    resp_lengths,
    cache_lengths,
    owner_slot,
    sink_count,
    window_size,
):
    tp_size = lax.axis_size("tp")
    tp_index = lax.axis_index("tp")
    local_reqs = queries.shape[1]
    local_heads = HEADS // tp_size
    group_size = HEADS // KV_HEADS
    kv_index = tp_index * local_heads // group_size
    cache_head = lax.dynamic_slice_in_dim(cache_kv, kv_index * HEAD, HEAD, axis=4)
    resp_head = lax.dynamic_slice_in_dim(response_kv, kv_index * HEAD, HEAD, axis=4)
    key_rows = jnp.concatenate([cache_head[:, :, 0], resp_head[:, :, 0]], axis=2)
    value_rows = jnp.concatenate([cache_head[:, :, 1], resp_head[:, :, 1]], axis=2)
    query_heads = queries.reshape(2, local_reqs, RESP, local_heads, HEAD)
    scores = jnp.einsum(
        "mrshd,mrkd->mrhsk", query_heads, key_rows, preferred_element_type=jnp.float32
    ) * HEAD ** (-0.5)
    allowed = span_mask(cache_lengths, sink_count, window_size)[None, :, None]
    masked = jnp.where(allowed, scores, -jnp.inf)
    row_peak = jnp.max(masked, axis=-1, keepdims=True)
    weights = jnp.exp(masked - row_peak)
    weights = (weights / jnp.sum(weights, axis=-1, keepdims=True)).astype(jnp.bfloat16)
    attended = jnp.einsum(
        "mrhsk,mrkd->mrshd", weights, value_rows, preferred_element_type=jnp.float32
    )
    attended = attended.astype(jnp.bfloat16).reshape(2, RESP, local_heads * HEAD)
    partial = jnp.einsum("msf,mfd->msd", attended, out_proj, preferred_element_type=jnp.float32)
    return fused_call(
        partial,
        residual.reshape(2, RESP, D),
        norm_gain,
        lm_head,
        targets,
        resp_lengths.reshape(1, REQS),
        owner_slot.reshape(1, REQS),
    )


def solution(mesh):
    in_specs = (
        P(None, "req", None, "tp"),
        P(None, "req", None, None, None),
        P(None, "req", None, None, None),
        P(None, "req", None, None),
        P(None, "tp", None),
        P(),
        P(None, "req", "tp"),
        P(None, "tp"),
        P(),
        P("req"),
        P(),
        P(),
        P(),
    )
    out_specs = (P("req", "tp"), P("req", None))
    return jax.shard_map(
        per_device, mesh=mesh, in_specs=in_specs, out_specs=out_specs, check_vma=False
    )
```

time: 1330 us -> 110 us (0.08)
  blocking collectives: 988 us -> 0 us
  waiting for transfers between devices: 281 us -> 0 us
  Pallas kernels: 0 us -> 100 us
  between operations: 19.9 us -> 2.78 us
  matrix products: 14.6 us -> 1.1 us
    psum x2 -> x0, blocking collectives: 500 us -> none  [the longest x1 491 us: per_device(): lax.psum((total_all * jnp.exp(peak_all - vocab_top), picked_all), 'req')]
    pmax x1 -> x0, blocking collectives: 488 us -> none  [per_device(): vocab_top = lax.pmax(peak_all, 'req')]
    all_gather x2 -> x0, waiting for transfers between devices: 220 us -> none  [the longest x1 150 us: per_device(): lax.all_gather(flat_rows, 'req', axis=1, tiled=True)]
    pallas_call x0 -> x1, Pallas kernels: none -> 100 us  [fused_call(): pl.pallas_call(fused, out_shape=(jax.ShapeDtypeStruct((1, 8), jnp.float32...]
    psum x1 -> x0, waiting for transfers between devices: 60.2 us -> none  [per_device(): lax.psum(partial_value, 'tp')]
    dot_general x2 -> x1, matrix products: 14 us -> 0.51 us  [per_device(): jnp.einsum('msf,mfd->msd', attended, out_proj, preferred_element_type=jnp...]
  transfers between devices with their start and end apart: 3 -> 0, of which waited for: 3 -> 0; matrix products, arithmetic and copies ran while one was open for 0% -> 0% of each run, Pallas kernels for 0% -> 0%
where the time goes in v1:
time: 110 us
  Pallas kernels  100 us (91%)
  local copies, waits for them, and re-layouts  5.45 us (5%)
  between operations  2.78 us (3%)
  matrix products  1.1 us (1%)
    pallas_call x1, Pallas kernels, fused_call(): pl.pallas_call(fused, out_shape=(jax.ShapeDtypeStruct((1, 8), jnp.float32...  100 us
    unnamed x17, local copies, waits for them, and re-layouts  2.57 us

profile of v1, /device:TPU:1, one launch (start us, length us, event | category | flops | bytes accessed | tf_op | source)
XLA Modules:
  0.0 109.7 jit_solution(600909009964105572)
XLA Ops:
  0.6 0.0 copy-start
  0.7 0.9 dynamic-slice_bitcast_fusion.2
  1.6 1.0 dynamic-slice_bitcast_fusion
  2.6 0.8 reshape.211
  5.5 0.1 fusion.10
  5.6 0.3 fusion.14
  5.9 0.2 fusion.3
  6.1 0.0 copy-start.6
  6.1 0.0 copy-start.2
  6.1 0.0 copy-start.3
  6.2 0.0 copy-start.4
  6.2 0.0 copy-start.5
  6.2 0.3 fusion.2
  6.5 0.1 reshape.213
  6.6 0.0 copy-done
  6.6 0.5 fusion.15.partial
  7.1 0.0 copy-done.6
  7.1 0.1 copy.23.targets
  7.2 0.0 copy-done.2
  7.2 0.0 copy-done.3
  7.2 0.0 copy-done.4
  7.2 0.0 copy-done.5
  7.2 0.0 copy-start.1
  7.2 1.4 %copy-done.1 = bf16[2,1024,384]{2,1,0:T(8,128)(2,1)S(1)} copy-done((bf16[2,1024,384]{2,1,0:T(8,128)(2,1)S(1)}, bf16[2,1024,384]{2,1,0:T(8,128)(2,1)}, u32[]{:S(2)}) %copy-start.1) | copy-done | bytes 1572888
  8.6 100.0 %shard_map.140 = (f32[1,8]{1,0:T(1,128)S(1)}, f32[1,2]{1,0:T(1,128)S(1)}) custom-call(f32[2,32,1536]{2,1,0:T(8,128)S(1)} %fusion.15.partial, bf16[2,32,1536]{2,1,0:T(8,128)(2,1)S(1)} %bitcast.61, f32[2,1536]{1,0:T(2,128)S(1)} %copy-done.3, bf16[2,1024,384]{2,1,0:T(8,128)(2,1)S(1)} %copy-done.1, s32[128,8]{1,0:T(8,128)S(1)} %copy.23.targets, ...), custom_call_target="tpu_custom_call" | custom-call | tf_op jit(solution)/shard_map/pallas_call | solution.py:424
  108.6 0.5 copy.41
  109.1 0.5 copy.42
  (8 shorter events, 0.1 us)
Async XLA Ops:
  0.6 5.9 %copy-start = (bf16[2,384,1536]{2,1,0:T(8,128)(2,1)S(1)}, bf16[2,384,1536]{2,1,0:T(8,128)(2,1)}, u32[]{:S(2)}) copy-start(bf16[2,384,1536]{2,1,0:T(8,128)(2,1)} %param.17) | copy-start | bytes 7077892
  6.1 1.0 copy-start.6
  6.1 1.1 copy-start.2
  6.1 1.1 copy-start.3
  6.2 1.1 copy-start.4
  6.2 1.0 copy-start.5
  7.2 1.4 %copy-start.1 = (bf16[2,1024,384]{2,1,0:T(8,128)(2,1)S(1)}, bf16[2,1024,384]{2,1,0:T(8,128)(2,1)}, u32[]{:S(2)}) copy-start(bf16[2,1024,384]{2,1,0:T(8,128)(2,1)} %head.1) | copy-start | bytes 4718596

commit v2 on v1

v2 whole, which is shorter than its diff:
```python
import jax
import jax.numpy as jnp
from jax import lax
from jax.experimental import pallas as pl
from jax.experimental.pallas import tpu as pltpu
from jax.sharding import PartitionSpec as P

HEADS = 12
HEAD = 128
KV_HEADS = 2
RESP = 32
CACHE = 384
KEYS = CACHE + RESP
D = 1536

NX, NZ, NC, NT = 4, 16, 2, 4
REQS = NX * NZ * NC
SLOTS = 16
FEAT = D // NT
GROUP = HEADS // NT
VOCAB_BLOCK = 1024
PIECES = 4
PIECE = VOCAB_BLOCK // PIECES
CHUNKS = 8
ROWS = 2 * NX * NC * SLOTS
SPLIT = 896
A = pl.ds(0, SPLIT)
B = pl.ds(SPLIT, D - SPLIT)
MESH = pl.DeviceIdType.MESH
EXACT = lax.Precision.HIGHEST


def iota(shape, dim):
    return lax.broadcasted_iota(jnp.int32, shape, dim)


def nt_dot(a, b, precision=None):
    return lax.dot_general(
        a, b, (((1,), (1,)), ((), ())), precision=precision, preferred_element_type=jnp.float32
    )


def fused(
    queries, response_kv, cache_kv, residual, out_proj, gain, head, targets, lengths, owner,
    cache_lengths, sink_count, window_size,
    policy_out, scores_out,
    qbuf, kvbuf, wbuf, resbuf, attbuf, partial,
    hbuf, rows, rs_in, tgt_in, tgt_all, own_all, wanted_buf, select_buf,
    peak_buf, norm_buf, pick_buf, outbuf, in1, ex2, in2, lpbuf, in3,
    load_sem, rs_s, rs_r, tg_s, tg_r, hp_s, hp_r, hq_s, hq_r, hf_s, hf_r,
    xa_s, xa_r, ra_s, ra_r, la_s, la_r, rb_s, rb_r, lb_s, lb_r, xb_s, xb_r,
    ca_s, ca_r, cb_s, cb_r, e1_s, e1_r, e2_s, e2_r, e3_s, e3_r,
):
    req = lax.axis_index("req")
    t = lax.axis_index("tp")
    x = req // (NZ * NC)
    z = (req // NC) % NZ
    c = req % NC
    model = t // 2
    half = t % 2
    pair = t + 1 - 2 * (t % 2)
    across = NT - 1 - t
    group = x * NC + c

    def index_of(px, pz, pc):
        return (px * NZ + pz) * NC + pc

    def send(src, dst, ssem, rsem, preq, pt):
        return pltpu.make_async_remote_copy(
            src_ref=src, dst_ref=dst, send_sem=ssem, recv_sem=rsem,
            device_id={"req": preq, "tp": pt}, device_id_type=MESH,
        )

    def lanes(source):
        return pl.ds(pl.multiple_of(source * FEAT, FEAT), FEAT)

    barrier = pltpu.get_barrier_semaphore()

    def greet(preq, pt):
        pl.semaphore_signal(
            barrier, inc=1, device_id={"req": preq, "tp": pt}, device_id_type=MESH
        )

    for d in range(1, NT):
        greet(req, (t + d) % NT)
    for d in range(1, NX * NC):
        other = (group + d) % (NX * NC)
        greet(index_of(other // NC, z, other % NC), t)
    for d in range(1, NZ):
        greet(index_of(x, (z + d) % NZ, c), t)

    kv_lanes = pl.ds(pl.multiple_of((t // 2) * HEAD, HEAD), HEAD)
    slot_start = pl.multiple_of(half * SLOTS, SLOTS)
    loads = [
        pltpu.make_async_copy(queries, qbuf, load_sem.at[0]),
        pltpu.make_async_copy(
            cache_kv.at[:, :, :, kv_lanes], kvbuf.at[:, :, pl.ds(0, CACHE)], load_sem.at[1]
        ),
        pltpu.make_async_copy(
            response_kv.at[:, :, :, kv_lanes], kvbuf.at[:, :, pl.ds(CACHE, RESP)], load_sem.at[2]
        ),
        pltpu.make_async_copy(out_proj, wbuf, load_sem.at[3]),
        pltpu.make_async_copy(residual.at[model, pl.ds(slot_start, SLOTS)], resbuf, load_sem.at[4]),
    ]
    own_head = pltpu.make_async_copy(head.at[model], hbuf.at[:, lanes(t)], load_sem.at[5])
    for copy in loads:
        copy.start()
    own_head.start()

    req_sub = iota((REQS, ROWS), 0)
    row_lane = iota((REQS, ROWS), 1)
    same_xc = ((req_sub >> 5) == (row_lane >> 6)) & ((req_sub & 1) == ((row_lane >> 4) & 1))
    same_z = ((iota((NZ, REQS), 1) >> 1) & (NZ - 1)) == iota((NZ, REQS), 0)
    zmask = jnp.where(same_z, 1.0, 0.0)

    pl.semaphore_wait(barrier, (NT - 1) + (NX * NC - 1) + (NZ - 1))

    def piece(k):
        return pl.ds(k * PIECE, PIECE)

    def pair_copy(k):
        return send(
            head.at[model, piece(k)], hbuf.at[piece(k), lanes(t)], hp_s.at[k], hp_r.at[k], req, pair
        )

    def across_copy(k):
        return send(
            head.at[1 - model, piece(k)], hbuf.at[piece(k), lanes(t)], hq_s.at[k], hq_r.at[k],
            req, across,
        )

    def across_recv(k):
        return send(
            head.at[1 - model, piece(k)], hbuf.at[piece(k), lanes(across)], hq_s.at[k], hq_r.at[k],
            req, across,
        )

    def forward_copy(k):
        part = hbuf.at[piece(k), lanes(across)]
        return send(part, part, hf_s.at[k], hf_r.at[k], req, pair)

    def pair_recv(k):
        part = hbuf.at[piece(k), lanes(pair)]
        return send(part, part, hp_s.at[k], hp_r.at[k], req, pair)

    def forward_recv(k):
        part = hbuf.at[piece(k), lanes(NT - 1 - pair)]
        return send(part, part, hf_s.at[k], hf_r.at[k], req, pair)

    across_copy(0).start()
    pair_copy(0).start()
    across_copy(1).start()

    for copy in loads[:3]:
        copy.wait()
    length = cache_lengths[0]
    stack = (GROUP * RESP, KEYS)
    query_pos = length + (iota(stack, 0) & (RESP - 1))
    key = iota(stack, 1)
    key_pos = jnp.where(key < CACHE, key, length + key - CACHE)
    key_live = (key >= CACHE) | (key < length)
    inside = (key_pos < sink_count[0]) | (query_pos - key_pos < window_size[0])
    allowed = key_live & (key_pos <= query_pos) & inside
    for m in range(2):
        stacked = jnp.concatenate(
            [qbuf[m, 0, :, HEAD * g : HEAD * g + HEAD] for g in range(GROUP)], axis=0
        )
        scores = nt_dot(stacked, kvbuf[m, 0]) * HEAD ** (-0.5)
        masked = jnp.where(allowed, scores, -jnp.inf)
        weights = jnp.exp(masked - jnp.max(masked, axis=-1, keepdims=True))
        weights = (weights / jnp.sum(weights, axis=-1, keepdims=True)).astype(jnp.bfloat16)
        attended = jnp.dot(weights, kvbuf[m, 1], preferred_element_type=jnp.float32)
        attended = attended.astype(jnp.bfloat16)
        for g in range(GROUP):
            attbuf[m, :, HEAD * g : HEAD * g + HEAD] = attended[RESP * g : RESP * g + RESP]
    loads[3].wait()
    for m in range(2):
        partial[m] = jnp.dot(attbuf[m], wbuf[m], preferred_element_type=jnp.float32)

    def rs_copy(d):
        pt = (t + d) % NT
        start = pl.multiple_of((pt % 2) * SLOTS, SLOTS)
        return send(
            partial.at[pt // 2, pl.ds(start, SLOTS)], rs_in.at[d], rs_s.at[d], rs_r.at[d], req, pt
        )

    for d in range(1, NT):
        rs_copy(d).start()

    spread = jnp.where(
        (iota((8, ROWS), 1) & (SLOTS - 1)) == iota((8, ROWS), 0) + 8 * half, 1.0, 0.0
    )
    wide = jnp.dot(
        targets[...].astype(jnp.float32), spread, precision=EXACT,
        preferred_element_type=jnp.float32,
    )
    placed = jnp.dot(
        zmask, jnp.where(same_xc, wide, 0.0), precision=EXACT, preferred_element_type=jnp.float32
    )
    tgt_in[0] = placed.astype(jnp.int32)

    def tgt_copy(d):
        return send(tgt_in.at[0], tgt_in.at[d], tg_s.at[d], tg_r.at[d], req, (t + d) % NT)

    for d in range(1, NT):
        tgt_copy(d).start()
    own_all[...] = jnp.dot(
        zmask * owner[...].astype(jnp.float32), jnp.where(same_xc, 1.0, 0.0), precision=EXACT,
        preferred_element_type=jnp.float32,
    ).astype(jnp.int32)

    def forward_head(k):
        across_recv(k).wait_recv()
        forward_copy(k).start()
        if k + 1 < PIECES:
            pair_copy(k + 1).start()

    across_copy(2).start()
    forward_head(0)
    across_copy(3).start()

    loads[4].wait()
    hidden = resbuf[...].astype(jnp.float32)
    total = partial[model, pl.ds(slot_start, SLOTS), :]
    for d in range(1, NT):
        rs_copy(d).wait_recv()
        total = total + rs_in[d]
    hidden = hidden + total
    scale_inv = lax.rsqrt(jnp.mean(hidden * hidden, axis=-1, keepdims=True) + 1e-06)
    rows[x, 7, 1, c] = (hidden * scale_inv * gain[pl.ds(model, 1), :]).astype(jnp.bfloat16)

    right = index_of(x, (z + 1) % NZ, c)
    left = index_of(x, (z + NZ - 1) % NZ, c)
    twin = index_of(x, z, 1 - c)

    def xa_copy(d):
        part = rows.at[x, 7, 1, c, :, A]
        return send(part, part, xa_s.at[d], xa_r.at[d], index_of((x + d) % NX, z, c), t)

    def xa_recv(d):
        part = rows.at[(x + NX - d) % NX, 7, 1, c, :, A]
        return send(part, part, xa_s.at[d], xa_r.at[d], index_of((x + d) % NX, z, c), t)

    def a_copy(side, s, h, first):
        src_chunk, src_place = (7, 1) if first else (s - 1, side)
        peers = pl.ds(2 * h, 2)
        ssem, rsem, to = (ra_s, ra_r, right) if side == 0 else (la_s, la_r, left)
        return send(
            rows.at[peers, src_chunk, src_place, c, :, A], rows.at[peers, s, side, c, :, A],
            ssem.at[2 * s + h], rsem.at[2 * s + h], to, t,
        )

    def b_copy(side, s, first):
        src_chunk, src_place = (7, 1) if first else (s - 1, side)
        ssem, rsem, to = (rb_s, rb_r, right) if side == 0 else (lb_s, lb_r, left)
        return send(
            rows.at[x, src_chunk, src_place, c, :, B], rows.at[x, s, side, c, :, B],
            ssem.at[s], rsem.at[s], to, t,
        )

    def xb_copy(n, d, side=None, chunk=None):
        place = pl.ds(0, 2) if side is None else pl.ds(side, 1)
        chunk = n if chunk is None else chunk
        part = rows.at[x, chunk, place, c, :, B]
        return send(
            part, part, xb_s.at[4 * n + d], xb_r.at[4 * n + d], index_of((x + d) % NX, z, c), t
        )

    def xb_recv(n, d, side=None, chunk=None):
        place = pl.ds(0, 2) if side is None else pl.ds(side, 1)
        chunk = n if chunk is None else chunk
        part = rows.at[(x + NX - d) % NX, chunk, place, c, :, B]
        return send(
            part, part, xb_s.at[4 * n + d], xb_r.at[4 * n + d], index_of((x + d) % NX, z, c), t
        )

    def twin_copy(n, ssem, rsem, part_lanes, side=None, chunk=None, core=None):
        place = pl.ds(0, 2) if side is None else pl.ds(side, 1)
        chunk = n if chunk is None else chunk
        core = c if core is None else core
        part = rows.at[:, chunk, place, core, :, part_lanes]
        return send(part, part, ssem.at[n], rsem.at[n], twin, t)

    def twin_a(n, **kw):
        return twin_copy(n, ca_s, ca_r, A, **kw)

    def twin_b(n, **kw):
        return twin_copy(n, cb_s, cb_r, B, **kw)

    OWN = dict(side=1, chunk=7)
    LAST = dict(side=0, chunk=7)

    for d in range(1, NX):
        xa_copy(d).start()
    b_copy(0, 0, True).start()
    b_copy(1, 0, True).start()
    for d in range(1, NX):
        xb_copy(8, d, **OWN).start()
    for d in range(1, NX):
        xa_recv(d).wait_recv()
    for h in range(2):
        a_copy(0, 0, h, True).start()
        a_copy(1, 0, h, True).start()
    twin_a(8, **OWN).start()
    forward_head(1)

    tgt_own = jnp.zeros((NZ, ROWS), jnp.int32)
    for d in range(NT):
        if d:
            tgt_copy(d).wait_recv()
        wanted_half = ((t + NT - d) % NT) // 2 == half
        tgt_own = tgt_own + jnp.where(wanted_half, tgt_in[d], 0)
    tgt_all[...] = tgt_own - req * VOCAB_BLOCK
    outbuf[...] = jnp.zeros_like(outbuf)
    peak_buf[...] = jnp.full_like(peak_buf, -jnp.inf)
    norm_buf[...] = jnp.zeros_like(norm_buf)
    pick_buf[...] = jnp.zeros_like(pick_buf)

    def prepare(k):
        z1 = (z + NZ - k - 1) % NZ
        z2 = (z + (k + 1) % 8) % NZ
        first = (iota((1, ROWS), 1) & 32) == 0
        wanted_buf[k] = jnp.where(first, tgt_all[pl.ds(z1, 1), :], tgt_all[pl.ds(z2, 1), :])
        sub = iota((REQS, ROWS), 0)
        dest = ((sub >> 5) * NZ + (sub & (NZ - 1))) * NC + ((sub >> 4) & 1)
        place = jnp.where(first, own_all[pl.ds(z1, 1), :], own_all[pl.ds(z2, 1), :])
        select_buf[k] = jnp.where(dest == place, 1.0, 0.0)

    def arrive(s):
        for side in range(2):
            if side == 1 and s == 8:
                continue
            for h in range(2):
                a_copy(side, s - 1, h, s == 1).wait_recv()
                if s < 8 - side:
                    a_copy(side, s, h, False).start()
            b_copy(side, s - 1, s == 1).wait_recv()
            if s < 8 - side:
                b_copy(side, s, False).start()

    def arrive_loop(s):
        for side in range(2):
            for h in range(2):
                a_copy(side, s - 1, h, False).wait_recv()
                a_copy(side, s, h, False).start()
            b_copy(side, s - 1, False).wait_recv()
            b_copy(side, s, False).start()

    def share(s):
        for d in range(1, NX):
            xb_copy(s - 1, d).start()
        twin_a(s - 1).start()

    def share_old(n, **kw):
        for d in range(1, NX):
            xb_recv(n, d, **kw).wait_recv()
        twin_b(n, **kw).start()

    arrive(1)
    share(1)
    share_old(8, **OWN)
    forward_head(2)
    prepare(0)
    prepare(1)

    arrive(2)
    share(2)
    share_old(0)
    forward_head(3)
    prepare(2)
    prepare(3)

    def middle(s, carry):
        arrive_loop(s)
        share(s)
        share_old(s - 2)
        prepare(2 * s - 2)
        prepare(2 * s - 1)
        return carry

    lax.fori_loop(3, 5, middle, 0)

    def other_core(n, **kw):
        twin_a(n, core=1 - c, **kw).wait_recv()
        twin_b(n, core=1 - c, **kw).wait_recv()

    def head_ready(k):
        pair_recv(k).wait_recv()
        forward_recv(k).wait_recv()

    def units(k0, k1, p0, p1):
        def unit(i, carry):
            k = k0 + i // (p1 - p0)
            p = p0 + i % (p1 - p0)
            base = pl.multiple_of(p * PIECE, PIECE)
            logits = nt_dot(hbuf[pl.ds(base, PIECE), :], rows[:, k].reshape(ROWS, D))
            peak = jnp.max(logits, axis=0, keepdims=True)
            hit = iota((PIECE, ROWS), 0) == wanted_buf[k] - base
            pick_buf[k] += jnp.sum(jnp.where(hit, logits, 0.0), axis=0, keepdims=True)
            old = peak_buf[k]
            new = jnp.maximum(old, peak)
            norm = jnp.sum(jnp.exp(logits - new), axis=0, keepdims=True)
            norm_buf[k] = norm_buf[k] * jnp.exp(old - new) + norm
            peak_buf[k] = new
            return carry

        lax.fori_loop(0, (k1 - k0) * (p1 - p0), unit, 0)

    arrive_loop(5)
    share(5)
    share_old(3)
    own_head.wait()
    head_ready(0)
    head_ready(1)
    for n in range(3):
        other_core(n)
    units(0, 3, 0, 2)

    arrive_loop(6)
    share(6)
    share_old(4)
    other_core(3)
    head_ready(2)
    units(3, 4, 0, 2)
    units(0, 4, 2, 3)

    arrive(7)
    share(7)
    share_old(5)
    other_core(4)
    units(4, 5, 0, 3)
    head_ready(3)
    units(0, 3, 3, 4)

    arrive(8)
    for d in range(1, NX):
        xb_copy(7, d, **LAST).start()
    twin_a(7, **LAST).start()
    share_old(6)
    other_core(5)
    units(5, 6, 0, 3)
    share_old(7, **LAST)
    units(3, 6, 3, 4)
    other_core(6)
    other_core(7, **LAST)
    other_core(8, **OWN)
    units(6, 8, 0, 4)

    def finish(k, carry):
        sub = iota((REQS, ROWS), 0)
        slot = iota((REQS, ROWS), 1) & (SLOTS - 1)
        lse = peak_buf[k] + jnp.log(norm_buf[k])
        values = jnp.where(sub == slot, lse, jnp.where(sub == slot + SLOTS, pick_buf[k], 0.0))
        outbuf[...] += nt_dot(select_buf[k], values, EXACT)
        return carry

    lax.fori_loop(0, CHUNKS, finish, 0)

    def e1_copy(d):
        other = (group + d) % (NX * NC)
        return send(
            outbuf.at[pl.ds(pl.multiple_of(other * NZ, NZ), NZ)], in1.at[d], e1_s.at[d], e1_r.at[d],
            index_of(other // NC, z, other % NC), t,
        )

    for d in range(1, NX * NC):
        e1_copy(d).start()
    in1[0] = outbuf[pl.ds(pl.multiple_of(group * NZ, NZ), NZ), :]
    for d in range(1, NX * NC):
        e1_copy(d).wait_recv()

    def combine(values):
        peak = jnp.max(values, axis=0, keepdims=True)
        lse = peak + jnp.log(jnp.sum(jnp.exp(values - peak), axis=0, keepdims=True))
        pick = jnp.sum(values, axis=0, keepdims=True)
        return jnp.where(iota(lse.shape, 2) < SLOTS, lse, pick)[0]

    merged = combine(in1[...])
    for k in range(NZ):
        ex2[k] = merged[k : k + 1]

    def e2_copy(d):
        pz = (z + d) % NZ
        return send(ex2.at[pz], in2.at[d], e2_s.at[d], e2_r.at[d], index_of(x, pz, c), t)

    for d in range(1, NZ):
        e2_copy(d).start()
    in2[0] = ex2[z]
    for d in range(1, NZ):
        e2_copy(d).wait_recv()
    final = combine(in2[...])
    logprob = pltpu.roll(final, 128 - SLOTS, 1) - final
    lpbuf[...] = logprob
    in3[t] = logprob

    def e3_copy(d):
        return send(lpbuf, in3.at[t], e3_s.at[d], e3_r.at[d], req, (t + d) % NT)

    def e3_recv(d):
        return send(lpbuf, in3.at[(t + NT - d) % NT], e3_s.at[d], e3_r.at[d], req, (t + d) % NT)

    for d in range(1, NT):
        e3_copy(d).start()
    count = jnp.sum(jnp.where(owner[...] == req, lengths[...], 0), axis=1, keepdims=True)
    for d in range(1, NT):
        e3_recv(d).wait_recv()
    lane = iota((1, 128), 1)
    live0 = (lane < SLOTS) & (lane < count)
    live1 = (lane < SLOTS) & (lane + SLOTS < count)
    low, high = in3[0], in3[1]
    policy_total = jnp.sum(
        jnp.where(live0, low, 0.0) + jnp.where(live1, high, 0.0), axis=1, keepdims=True
    )
    ratio_total = jnp.sum(
        jnp.where(live0, low - in3[2], 0.0) + jnp.where(live1, high - in3[3], 0.0),
        axis=1, keepdims=True,
    )
    counts = count.astype(jnp.float32)
    scores = jnp.where(lane == 0, policy_total / counts, ratio_total / counts)
    scores_out[...] = scores[:, 0:2]
    mine = in3[t // 2]
    mine = jnp.where(half == 1, pltpu.roll(mine, 120, 1), mine)
    mine = jnp.where(lane + 8 * t < count, mine, 0.0)
    policy_out[...] = mine[:, 0:8]

    for d in range(1, NT):
        rs_copy(d).wait_send()
        tgt_copy(d).wait_send()
        e3_copy(d).wait_send()
    for d in range(1, NX):
        xa_copy(d).wait_send()
        xb_copy(8, d, **OWN).wait_send()
        xb_copy(7, d, **LAST).wait_send()
    twin_a(8, **OWN).wait_send()
    twin_b(8, **OWN).wait_send()
    twin_a(7, **LAST).wait_send()
    twin_b(7, **LAST).wait_send()

    def sent(n, carry):
        for d in range(1, NX):
            xb_copy(n, d).wait_send()
        twin_a(n).wait_send()
        twin_b(n).wait_send()
        return carry

    lax.fori_loop(0, 7, sent, 0)

    def head_sent(k, carry):
        pair_copy(k).wait_send()
        across_copy(k).wait_send()
        forward_copy(k).wait_send()
        return carry

    lax.fori_loop(0, PIECES, head_sent, 0)

    def ring_sent(side, s, first):
        for h in range(2):
            a_copy(side, s, h, first).wait_send()
        b_copy(side, s, first).wait_send()

    for side in range(2):
        ring_sent(side, 0, True)

        def side_sent(s, carry):
            ring_sent(side, s, False)
            return carry

        lax.fori_loop(1, 8 - side, side_sent, 0)
    for d in range(1, NX * NC):
        e1_copy(d).wait_send()
    for d in range(1, NZ):
        e2_copy(d).wait_send()


def per_device(
    queries,
    response_kv,
    cache_kv,
    residual,
    out_proj,
    norm_gain,
    lm_head,
    targets,
    resp_lengths,
    cache_lengths,
    owner_slot,
    sink_count,
    window_size,
):
    dma = pltpu.SemaphoreType.DMA
    vmem = pl.BlockSpec(memory_space=pltpu.VMEM)
    hbm = pl.BlockSpec(memory_space=pltpu.HBM)
    smem = pl.BlockSpec(memory_space=pltpu.SMEM)
    semaphores = [6] + [NT] * 4 + [PIECES] * 6 + [NX] * 2 + [16] * 4 + [8] * 4 + [36] * 2
    semaphores += [9] * 4 + [8] * 2 + [NZ] * 2 + [NT] * 2
    bf16, f32, i32 = jnp.bfloat16, jnp.float32, jnp.int32
    return pl.pallas_call(
        fused,
        out_shape=(jax.ShapeDtypeStruct((1, 8), f32), jax.ShapeDtypeStruct((1, 2), f32)),
        in_specs=[hbm] * 5 + [vmem, hbm] + [vmem] * 3 + [smem] * 3,
        out_specs=(vmem, vmem),
        scratch_shapes=[
            pltpu.VMEM((2, 1, RESP, FEAT), bf16),
            pltpu.VMEM((2, 2, KEYS, HEAD), bf16),
            pltpu.VMEM((2, FEAT, D), bf16),
            pltpu.VMEM((SLOTS, D), bf16),
            pltpu.VMEM((2, RESP, FEAT), bf16),
            pltpu.VMEM((2, RESP, D), f32),
            pltpu.VMEM((VOCAB_BLOCK, D), bf16),
            pltpu.VMEM((NX, CHUNKS, 2, NC, SLOTS, D), bf16),
            pltpu.VMEM((NT, SLOTS, D), f32),
            pltpu.VMEM((NT, NZ, ROWS), i32),
            pltpu.VMEM((NZ, ROWS), i32),
            pltpu.VMEM((NZ, ROWS), i32),
            pltpu.VMEM((CHUNKS, 1, ROWS), i32),
            pltpu.VMEM((CHUNKS, REQS, ROWS), f32),
            pltpu.VMEM((CHUNKS, 1, ROWS), f32),
            pltpu.VMEM((CHUNKS, 1, ROWS), f32),
            pltpu.VMEM((CHUNKS, 1, ROWS), f32),
            pltpu.VMEM((REQS, 128), f32),
            pltpu.VMEM((NX * NC, NZ, 128), f32),
            pltpu.VMEM((NZ, 1, 128), f32),
            pltpu.VMEM((NZ, 1, 128), f32),
            pltpu.VMEM((1, 128), f32),
            pltpu.VMEM((NT, 1, 128), f32),
        ]
        + [dma((n,)) for n in semaphores],
        compiler_params=pltpu.CompilerParams(
            collective_id=0, has_side_effects=True, vmem_limit_bytes=48 << 20
        ),
    )(
        queries,
        response_kv.reshape(2, 2, RESP, KV_HEADS * HEAD),
        cache_kv.reshape(2, 2, CACHE, KV_HEADS * HEAD),
        residual.reshape(2, RESP, D),
        out_proj,
        norm_gain,
        lm_head,
        targets,
        resp_lengths.reshape(1, REQS),
        owner_slot.reshape(1, REQS),
        cache_lengths,
        sink_count,
        window_size,
    )


def solution(mesh):
    in_specs = (
        P(None, "req", None, "tp"),
        P(None, "req", None, None, None),
        P(None, "req", None, None, None),
        P(None, "req", None, None),
        P(None, "tp", None),
        P(),
        P(None, "req", "tp"),
        P(None, "tp"),
        P(),
        P("req"),
        P(),
        P(),
        P(),
    )
    out_specs = (P("req", "tp"), P("req", None))
    return jax.shard_map(
        per_device, mesh=mesh, in_specs=in_specs, out_specs=out_specs, check_vma=False
    )
```

time: 110 us -> 111 us (level)
  local copies, waits for them, and re-layouts: 5.45 us -> 10.6 us
  Pallas kernels: 100 us -> 97.2 us
    unnamed x17 -> x21, local copies, waits for them, and re-layouts: 2.57 us -> 10.6 us
    pallas_call x1, Pallas kernels: 100 us -> 97.2 us  [per_device(): pl.pallas_call(fused, out_shape=(jax.ShapeDtypeStruct((1, 8), f32), jax.S...]
    squeeze x2 -> x0, local copies, waits for them, and re-layouts: 1.95 us -> none  [the longest x1 1.05 us: per_device(): cache_head[:, :, 0]]
where the time goes in v2:
time: 111 us; the launch traced here: 110 us
  Pallas kernels  97.2 us (88%)
  local copies, waits for them, and re-layouts  10.6 us (10%)
  between operations  2.59 us (2%)
    pallas_call x1, Pallas kernels, per_device(): pl.pallas_call(fused, out_shape=(jax.ShapeDtypeStruct((1, 8), f32), jax.S...  97.2 us
    unnamed x21, local copies, waits for them, and re-layouts  10.6 us

profile of v2, /device:TPU:1, one launch (start us, length us, event | category | flops | bytes accessed | tf_op | source)
XLA Modules:
  0.0 110.4 jit_solution(13089569582294048155)
XLA Ops:
  2.6 0.8 copy.15.targets
  3.4 0.0 copy-start
  3.4 1.7 %copy-done = bf16[2,384,1536]{2,1,0:T(8,128)(2,1)S(1)} copy-done((bf16[2,384,1536]{2,1,0:T(8,128)(2,1)S(1)}, bf16[2,384,1536]{2,1,0:T(8,128)(2,1)}, u32[]{:S(2)}) %copy-start) | copy-done | bytes 2359320
  5.0 0.0 copy-start.1
  5.0 1.4 %copy-done.1 = bf16[2,1024,384]{2,1,0:T(8,128)(2,1)S(1)} copy-done((bf16[2,1024,384]{2,1,0:T(8,128)(2,1)S(1)}, bf16[2,1024,384]{2,1,0:T(8,128)(2,1)}, u32[]{:S(2)}) %copy-start.1) | copy-done | bytes 1572888
  6.4 0.0 copy-start.2
  6.4 1.1 %copy-done.2 = bf16[2,1,2,384,256]{4,3,2,1,0:T(8,128)(2,1)S(1)} copy-done((bf16[2,1,2,384,256]{4,3,2,1,0:T(8,128)(2,1)S(1)}, bf16[2,1,2,384,256]{4,3,2,1,0:T(8,128)(2,1)}, u32[]{:S(2)}) %copy-start.2) | copy-done | bytes 786456
  7.6 0.0 copy-start.3
  7.6 0.9 copy-done.3
  8.5 0.0 copy-start.4
  8.5 0.8 copy-done.4
  9.3 0.0 copy-start.5
  9.3 0.8 copy-done.5
  10.1 0.0 copy-start.6
  10.1 0.7 copy-done.6
  10.8 0.0 copy-start.7
  10.8 0.7 copy-done.7
  11.5 0.0 copy-start.8
  11.5 0.7 copy-done.8
  12.1 97.2 %shard_map.140 = (f32[1,8]{1,0:T(1,128)S(1)}, f32[1,2]{1,0:T(1,128)S(1)}) custom-call(bf16[2,1,32,384]{3,2,1,0:T(8,128)(2,1)S(1)} %copy-done.5, bf16[2,2,32,256]{3,2,1,0:T(8,128)(2,1)S(1)} %bitcast.7, bf16[2,2,384,256]{3,2,1,0:T(8,128)(2,1)S(1)} %bitcast.5, bf16[2,32,1536]{2,1,0:T(8,128)(2,1)S(1)} %bitcast.6, bf16[2,384,1536]{2,1,0:T(8,128)(2,1)S(1)} %copy-done, ...), custom_call_target="tpu_custom_call" | custom-call | tf_op jit(solution)/shard_map/pallas_call | solution.py:597
  109.3 0.5 copy.21
  109.8 0.5 copy.22
Async XLA Ops:
  3.4 1.7 %copy-start = (bf16[2,384,1536]{2,1,0:T(8,128)(2,1)S(1)}, bf16[2,384,1536]{2,1,0:T(8,128)(2,1)}, u32[]{:S(2)}) copy-start(bf16[2,384,1536]{2,1,0:T(8,128)(2,1)} %out_proj.1) | copy-start | bytes 7077892
  5.0 1.4 %copy-start.1 = (bf16[2,1024,384]{2,1,0:T(8,128)(2,1)S(1)}, bf16[2,1024,384]{2,1,0:T(8,128)(2,1)}, u32[]{:S(2)}) copy-start(bf16[2,1024,384]{2,1,0:T(8,128)(2,1)} %head.1) | copy-start | bytes 4718596
  6.4 1.1 %copy-start.2 = (bf16[2,1,2,384,256]{4,3,2,1,0:T(8,128)(2,1)S(1)}, bf16[2,1,2,384,256]{4,3,2,1,0:T(8,128)(2,1)}, u32[]{:S(2)}) copy-start(bf16[2,1,2,384,256]{4,3,2,1,0:T(8,128)(2,1)} %param.15) | copy-start | bytes 2359300
  7.6 0.9 copy-start.3
  8.5 0.8 copy-start.4
  9.3 0.8 copy-start.5
  10.1 0.7 copy-start.6
  10.8 0.7 copy-start.7
  11.5 0.7 copy-start.8

commit v3 on v2

v3 whole, which is shorter than its diff:
```python
import jax
import jax.numpy as jnp
from jax import lax
from jax.experimental import pallas as pl
from jax.experimental.pallas import tpu as pltpu
from jax.sharding import PartitionSpec as P

HEADS = 12
HEAD = 128
KV_HEADS = 2
RESP = 32
CACHE = 384
KEYS = CACHE + RESP
D = 1536

NX, NZ, NC, NT = 4, 16, 2, 4
REQS = NX * NZ * NC
SLOTS = 16
FEAT = D // NT
GROUP = HEADS // NT
VOCAB_BLOCK = 1024
PIECES = 4
PIECE = VOCAB_BLOCK // PIECES
CHUNKS = 8
ROWS = 2 * NX * NC * SLOTS
SPLIT = 128
MIDDLE = SPLIT + 768
A = pl.ds(0, SPLIT)
B = pl.ds(SPLIT, D - SPLIT)
B_PARTS = (pl.ds(SPLIT, MIDDLE - SPLIT), pl.ds(MIDDLE, D - MIDDLE))
OWN = 4 * 4 - 1
MESH = pl.DeviceIdType.MESH
EXACT = lax.Precision.HIGHEST


def iota(shape, dim):
    return lax.broadcasted_iota(jnp.int32, shape, dim)


def nt_dot(a, b, precision=None):
    return lax.dot_general(
        a, b, (((1,), (1,)), ((), ())), precision=precision, preferred_element_type=jnp.float32
    )


def fused(
    queries, response_kv, cache_kv, residual, out_proj, gain_in, head, targets_in, lengths_in,
    owner_in, cache_lengths_in, sink_count_in, window_size_in,
    policy_out, scores_out,
    gain, targets, lengths, owner, cache_lengths, sink_count, window_size,
    qbuf, kvbuf, wbuf, resbuf, attbuf, partial,
    hbuf, rows, rs_in, tgt_in, tgt_all, own_all, wanted_buf, select_buf,
    peak_buf, norm_buf, pick_buf, outbuf, in1, ex2, in2, in3,
    load_sem, rs_s, rs_r, tg_s, tg_r, hp_s, hp_r, hq_s, hq_r, hf_s, hf_r,
    xa_s, xa_r, za_s, za_r, zb_s, zb_r, xb_s, xb_r, c_s, c_r, e1_s, e1_r, e2_s, e2_r,
):
    req = lax.axis_index("req")
    t = lax.axis_index("tp")
    x = req // (NZ * NC)
    z = (req // NC) % NZ
    c = req % NC
    model = t // 2
    half = t % 2
    pair = t + 1 - 2 * (t % 2)
    across = NT - 1 - t
    group = x * NC + c

    def index_of(px, pz, pc):
        return (px * NZ + pz) * NC + pc

    def send(src, dst, ssem, rsem, preq, pt):
        return pltpu.make_async_remote_copy(
            src_ref=src, dst_ref=dst, send_sem=ssem, recv_sem=rsem,
            device_id={"req": preq, "tp": pt}, device_id_type=MESH,
        )

    def lanes(source):
        return pl.ds(pl.multiple_of(source * FEAT, FEAT), FEAT)

    barrier = pltpu.get_barrier_semaphore()

    def greet(preq, pt):
        pl.semaphore_signal(
            barrier, inc=1, device_id={"req": preq, "tp": pt}, device_id_type=MESH
        )

    for d in range(1, NX * NC):
        other = (group + d) % (NX * NC)
        greet(index_of(other // NC, z, other % NC), t)
    for d in range(1, NT):
        greet(req, (t + d) % NT)

    def greet_ring(d, carry):
        for e in range(NT):
            greet(index_of(x, (z + d) % NZ, c), (t + e) % NT)
        return carry

    lax.fori_loop(1, NZ, greet_ring, 0)

    kv_lanes = pl.ds(pl.multiple_of((t // 2) * HEAD, HEAD), HEAD)
    slot_start = pl.multiple_of(half * SLOTS, SLOTS)
    loads = [
        pltpu.make_async_copy(queries, qbuf, load_sem.at[0]),
        pltpu.make_async_copy(
            cache_kv.at[:, :, :, kv_lanes], kvbuf.at[:, :, pl.ds(0, CACHE)], load_sem.at[1]
        ),
        pltpu.make_async_copy(
            response_kv.at[:, :, :, kv_lanes], kvbuf.at[:, :, pl.ds(CACHE, RESP)], load_sem.at[2]
        ),
        pltpu.make_async_copy(out_proj, wbuf, load_sem.at[3]),
        pltpu.make_async_copy(residual.at[model, pl.ds(slot_start, SLOTS)], resbuf, load_sem.at[4]),
    ]
    small = [
        (cache_lengths_in, cache_lengths), (sink_count_in, sink_count),
        (window_size_in, window_size), (targets_in, targets), (owner_in, owner),
        (lengths_in, lengths), (gain_in, gain),
    ]
    small = [
        pltpu.make_async_copy(src, dst, load_sem.at[6 + i]) for i, (src, dst) in enumerate(small)
    ]
    own_head = pltpu.make_async_copy(head.at[model], hbuf.at[:, lanes(t)], load_sem.at[5])
    for copy in small + loads:
        copy.start()
    own_head.start()

    req_sub = iota((REQS, ROWS), 0)
    row_lane = iota((REQS, ROWS), 1)
    same_xc = ((req_sub >> 5) == (row_lane >> 6)) & ((req_sub & 1) == ((row_lane >> 4) & 1))
    same_z = ((iota((NZ, REQS), 1) >> 1) & (NZ - 1)) == iota((NZ, REQS), 0)
    zmask = jnp.where(same_z, 1.0, 0.0)

    pl.semaphore_wait(barrier, (NX * NC - 1) + (NT * NZ - 1))

    def piece(k):
        return pl.ds(k * PIECE, PIECE)

    def pair_copy(k):
        return send(
            head.at[model, piece(k)], hbuf.at[piece(k), lanes(t)], hp_s.at[k], hp_r.at[k], req, pair
        )

    def across_copy(k):
        return send(
            head.at[1 - model, piece(k)], hbuf.at[piece(k), lanes(t)], hq_s.at[k], hq_r.at[k],
            req, across,
        )

    def across_recv(k):
        return send(
            head.at[1 - model, piece(k)], hbuf.at[piece(k), lanes(across)], hq_s.at[k], hq_r.at[k],
            req, across,
        )

    def forward_copy(k):
        part = hbuf.at[piece(k), lanes(across)]
        return send(part, part, hf_s.at[k], hf_r.at[k], req, pair)

    def pair_recv(k):
        part = hbuf.at[piece(k), lanes(pair)]
        return send(part, part, hp_s.at[k], hp_r.at[k], req, pair)

    def forward_recv(k):
        part = hbuf.at[piece(k), lanes(NT - 1 - pair)]
        return send(part, part, hf_s.at[k], hf_r.at[k], req, pair)

    across_copy(0).start()
    pair_copy(0).start()
    across_copy(1).start()

    for copy in small + loads[:3]:
        copy.wait()
    length = cache_lengths[...]
    stack = (GROUP * RESP, KEYS)
    query_pos = length + (iota(stack, 0) & (RESP - 1))
    key = iota(stack, 1)
    key_pos = jnp.where(key < CACHE, key, length + key - CACHE)
    key_live = (key >= CACHE) | (key < length)
    inside = (key_pos < sink_count[...]) | (query_pos - key_pos < window_size[...])
    allowed = key_live & (key_pos <= query_pos) & inside
    for m in range(2):
        stacked = jnp.concatenate(
            [qbuf[m, 0, :, HEAD * g : HEAD * g + HEAD] for g in range(GROUP)], axis=0
        )
        scores = nt_dot(stacked, kvbuf[m, 0]) * HEAD ** (-0.5)
        masked = jnp.where(allowed, scores, -jnp.inf)
        weights = jnp.exp(masked - jnp.max(masked, axis=-1, keepdims=True))
        weights = (weights / jnp.sum(weights, axis=-1, keepdims=True)).astype(jnp.bfloat16)
        attended = jnp.dot(weights, kvbuf[m, 1], preferred_element_type=jnp.float32)
        attended = attended.astype(jnp.bfloat16)
        for g in range(GROUP):
            attbuf[m, :, HEAD * g : HEAD * g + HEAD] = attended[RESP * g : RESP * g + RESP]
    loads[3].wait()
    for m in range(2):
        partial[m] = jnp.dot(attbuf[m], wbuf[m], preferred_element_type=jnp.float32)

    def rs_copy(d):
        pt = (t + d) % NT
        start = pl.multiple_of((pt % 2) * SLOTS, SLOTS)
        return send(
            partial.at[pt // 2, pl.ds(start, SLOTS)], rs_in.at[d], rs_s.at[d], rs_r.at[d], req, pt
        )

    for d in range(1, NT):
        rs_copy(d).start()

    same_xc_wide = jnp.where(same_xc, 1.0, 0.0)
    wide = jnp.concatenate(
        [zmask * targets[s : s + 1, :].astype(jnp.float32) for s in range(8)], axis=0
    )
    wide = jnp.dot(wide, same_xc_wide, precision=EXACT, preferred_element_type=jnp.float32)
    slot_lane = iota((NZ, ROWS), 1) & (SLOTS - 1)
    placed = jnp.zeros((NZ, ROWS), jnp.float32)
    for s in range(8):
        placed = jnp.where(slot_lane == s + 8 * half, wide[NZ * s : NZ * s + NZ], placed)
    tgt_in[0] = placed.astype(jnp.int32)

    def tgt_copy(d):
        return send(tgt_in.at[0], tgt_in.at[d], tg_s.at[d], tg_r.at[d], req, (t + d) % NT)

    for d in range(1, NT):
        tgt_copy(d).start()
    own_all[...] = jnp.dot(
        zmask * owner[...].astype(jnp.float32), same_xc_wide, precision=EXACT,
        preferred_element_type=jnp.float32,
    ).astype(jnp.int32)

    def forward_head(k):
        across_recv(k).wait_recv()
        forward_copy(k).start()
        if k + 1 < PIECES:
            pair_copy(k + 1).start()

    across_copy(2).start()
    forward_head(0)
    across_copy(3).start()

    loads[4].wait()
    hidden = resbuf[...].astype(jnp.float32)
    total = partial[model, pl.ds(slot_start, SLOTS), :]
    for d in range(1, NT):
        rs_copy(d).wait_recv()
        total = total + rs_in[d]
    hidden = hidden + total
    scale_inv = lax.rsqrt(jnp.mean(hidden * hidden, axis=-1, keepdims=True) + 1e-06)
    rows[x, OWN, c] = (hidden * scale_inv * gain[pl.ds(model, 1), :]).astype(jnp.bfloat16)

    steps = range(1, 5)
    streams = [(side, j) for side in range(2) for j in range(2)]

    def slot_of(k, side, j):
        return 4 * (k - 1) + 2 * side + j

    def exists(k, side, j):
        return slot_of(k, side, j) != OWN

    def away(side, hops):
        return index_of(x, (z + hops) % NZ if side == 0 else (z + NZ - hops) % NZ, c)

    targets_of = [[away(side, 1), away(side, 2)] for side in range(2)]

    def z_copy(part_a, k, side, j):
        src = OWN if k == 1 else slot_of(k - 1, side, j)
        dst = slot_of(k, side, j)
        to = targets_of[side][j if k == 1 else 1]
        if part_a:
            return send(
                rows.at[:, src, c, :, A], rows.at[:, dst, c, :, A], za_s.at[dst], za_r.at[dst], to, t
            )
        return send(
            rows.at[x, src, c, :, B], rows.at[x, dst, c, :, B], zb_s.at[dst], zb_r.at[dst], to, t
        )

    beside = [index_of((x + d) % NX, z, c) for d in range(NX)]
    twin = index_of(x, z, 1 - c)

    def xa_copy(d):
        part = rows.at[x, OWN, c, :, A]
        return send(part, part, xa_s.at[d], xa_r.at[d], beside[d], t)

    def xa_recv(d):
        part = rows.at[(x + NX - d) % NX, OWN, c, :, A]
        return send(part, part, xa_s.at[d], xa_r.at[d], beside[d], t)

    groups = [(OWN, 1)] + [(4 * (k - 1) + 2 * side, 2) for k in steps for side in range(2)]
    groups[8] = (OWN - 1, 1)

    def x_part(g, block, part_lanes):
        start, size = groups[g]
        return rows.at[(x + block) % NX, pl.ds(start, size), c, :, part_lanes]

    def x_copy(g, way, second, receiving=False):
        back = NX - 1 if way == 0 else 1
        block = (back if second else 0) + (back if receiving else 0)
        part = x_part(g, block, B_PARTS[way] if second else B)
        n = 4 * g + 2 * second + way
        return send(part, part, xb_s.at[n], xb_r.at[n], beside[1 if way == 0 else NX - 1], t)

    def twin_copy(g, core):
        start, size = groups[g]
        part = rows.at[:, pl.ds(start, size), core]
        return send(part, part, c_s.at[g], c_r.at[g], twin, t)

    def x_send(g):
        for way in range(2):
            x_copy(g, way, 0).start()

    def x_pass(g):
        for way in range(2):
            x_copy(g, way, 0, True).wait_recv()
            x_copy(g, way, 1).start()

    def x_done(g):
        for way in range(2):
            x_copy(g, way, 1, True).wait_recv()
        twin_copy(g, c).start()

    def other_core(*gs):
        for g in gs:
            twin_copy(g, 1 - c).wait_recv()

    def arrive(k):
        for side in range(2):
            for j in range(2):
                if not exists(k, side, j):
                    continue
                for part_a in (True, False):
                    z_copy(part_a, k, side, j).wait_recv()
                    if k < 4 and exists(k + 1, side, j):
                        z_copy(part_a, k + 1, side, j).start()
            x_send(2 * k - 1 + side)

    for d in range(1, NX):
        xa_copy(d).start()
    for j in range(2):
        for side in range(2):
            z_copy(False, 1, side, j).start()
    x_send(0)
    for d in range(1, NX):
        xa_recv(d).wait_recv()
    for j in range(2):
        for side in range(2):
            z_copy(True, 1, side, j).start()
    forward_head(1)

    tgt_own = jnp.zeros((NZ, ROWS), jnp.int32)
    for d in range(NT):
        if d:
            tgt_copy(d).wait_recv()
        wanted_half = ((t + NT - d) % NT) // 2 == half
        tgt_own = tgt_own + jnp.where(wanted_half, tgt_in[d], 0)
    tgt_all[...] = tgt_own - req * VOCAB_BLOCK
    outbuf[...] = jnp.zeros_like(outbuf)
    peak_buf[...] = jnp.full_like(peak_buf, -jnp.inf)
    norm_buf[...] = jnp.zeros_like(norm_buf)
    pick_buf[...] = jnp.zeros_like(pick_buf)

    def prepare(n):
        if n % 2 == 0:
            z1, z2 = (z + NZ - n - 1) % NZ, (z + NZ - n - 2) % NZ
        else:
            z1, z2 = (z + n) % NZ, (z + (n + 1) % 8) % NZ
        first = (iota((1, ROWS), 1) & 32) == 0
        wanted_buf[n] = jnp.where(first, tgt_all[pl.ds(z1, 1), :], tgt_all[pl.ds(z2, 1), :])
        sub = iota((REQS, ROWS), 0)
        dest = ((sub >> 5) * NZ + (sub & (NZ - 1))) * NC + ((sub >> 4) & 1)
        place = jnp.where(first, own_all[pl.ds(z1, 1), :], own_all[pl.ds(z2, 1), :])
        select_buf[n] = jnp.where(dest == place, 1.0, 0.0).astype(jnp.bfloat16)

    def head_ready(k):
        pair_recv(k).wait_recv()
        forward_recv(k).wait_recv()

    def units(k0, k1, p0, p1):
        def unit(i, carry):
            k = k0 + i // (p1 - p0)
            p = p0 + i % (p1 - p0)
            base = pl.multiple_of(p * PIECE, PIECE)
            chunk = rows[:, pl.ds(2 * k, 2)].reshape(ROWS, D)
            logits = nt_dot(hbuf[pl.ds(base, PIECE), :], chunk)
            peak = jnp.max(logits, axis=0, keepdims=True)
            hit = iota((PIECE, ROWS), 0) == wanted_buf[k] - base
            pick_buf[k] += jnp.sum(jnp.where(hit, logits, 0.0), axis=0, keepdims=True)
            old = peak_buf[k]
            new = jnp.maximum(old, peak)
            norm = jnp.sum(jnp.exp(logits - new), axis=0, keepdims=True)
            norm_buf[k] = norm_buf[k] * jnp.exp(old - new) + norm
            peak_buf[k] = new
            return carry

        lax.fori_loop(0, (k1 - k0) * (p1 - p0), unit, 0)

    x_pass(0)
    arrive(1)
    forward_head(2)
    for n in range(4):
        prepare(n)
    x_done(0)

    x_pass(1)
    x_pass(2)
    arrive(2)
    forward_head(3)
    x_done(1)
    x_done(2)
    for n in range(4, CHUNKS):
        prepare(n)

    x_pass(3)
    x_pass(4)
    arrive(3)
    x_done(3)
    x_done(4)
    own_head.wait()
    head_ready(0)
    head_ready(1)
    other_core(1, 2)
    units(0, 2, 0, 2)

    x_pass(5)
    x_pass(6)
    arrive(4)
    x_done(5)
    x_done(6)
    other_core(3, 4)
    units(2, 4, 0, 2)
    x_pass(7)
    x_pass(8)
    head_ready(2)
    units(0, 4, 2, 3)
    head_ready(3)
    units(0, 4, 3, 4)
    other_core(5, 6)
    units(4, 6, 0, 2)
    x_done(7)
    x_done(8)
    units(4, 6, 2, 4)
    other_core(7, 8, 0)
    units(6, 8, 0, 4)

    def finish(k, carry):
        sub = iota((2 * SLOTS, ROWS), 0)
        slot = iota((2 * SLOTS, ROWS), 1) & (SLOTS - 1)
        lse = peak_buf[k] + jnp.log(norm_buf[k])
        values = jnp.where(sub == slot, lse, jnp.where(sub == slot + SLOTS, pick_buf[k], 0.0))
        terms = []
        for _ in range(3):
            terms.append(values.astype(jnp.bfloat16))
            values = values - terms[-1].astype(jnp.float32)
        terms.append(jnp.zeros_like(terms[0]))
        outbuf[...] += nt_dot(select_buf[k], jnp.concatenate(terms, axis=0))
        return carry

    lax.fori_loop(0, CHUNKS, finish, 0)
    found = outbuf[...]
    outbuf[...] = (found + pltpu.roll(found, 96, 1)) + pltpu.roll(found, 64, 1)

    def e1_copy(d):
        other = (group + d) % (NX * NC)
        return send(
            outbuf.at[pl.ds(pl.multiple_of(other * NZ, NZ), NZ)], in1.at[d], e1_s.at[d], e1_r.at[d],
            index_of(other // NC, z, other % NC), t,
        )

    for d in range(1, NX * NC):
        e1_copy(d).start()
    in1[0] = outbuf[pl.ds(pl.multiple_of(group * NZ, NZ), NZ), :]
    for d in range(1, NX * NC):
        e1_copy(d).wait_recv()

    def combine(values):
        peak = jnp.max(values, axis=0, keepdims=True)
        lse = peak + jnp.log(jnp.sum(jnp.exp(values - peak), axis=0, keepdims=True))
        pick = jnp.sum(values, axis=0, keepdims=True)
        return jnp.where(iota(lse.shape, 2) < SLOTS, lse, pick)[0]

    merged = combine(in1[...])
    for k in range(NZ):
        ex2[k] = merged[k : k + 1]

    def e2_copy(d, e):
        pz = (z + d) % NZ
        n = NT * d + e
        return send(
            ex2.at[pz], in2.at[t, d], e2_s.at[n], e2_r.at[n], index_of(x, pz, c), (t + e) % NT
        )

    def e2_recv(d, e):
        n = NT * d + e
        dst = in2.at[(t + NT - e) % NT, d]
        return send(ex2.at[0], dst, e2_s.at[n], e2_r.at[n], index_of(x, (z + d) % NZ, c), (t + e) % NT)

    def ring_loop(body):
        def step(d, carry):
            for e in range(NT):
                body(d, e)
            return carry

        for e in range(1, NT):
            body(0, e)
        lax.fori_loop(1, NZ, step, 0)

    ring_loop(lambda d, e: e2_copy(d, e).start())
    in2[t, 0] = ex2[z]
    count = jnp.sum(jnp.where(owner[...] == req, lengths[...], 0), axis=1, keepdims=True)
    ring_loop(lambda d, e: e2_recv(d, e).wait_recv())
    for column in range(NT):
        final = combine(in2[column])
        in3[column] = pltpu.roll(final, 128 - SLOTS, 1) - final
    lane = iota((1, 128), 1)
    live0 = (lane < SLOTS) & (lane < count)
    live1 = (lane < SLOTS) & (lane + SLOTS < count)
    low, high = in3[0], in3[1]
    policy_total = jnp.sum(
        jnp.where(live0, low, 0.0) + jnp.where(live1, high, 0.0), axis=1, keepdims=True
    )
    ratio_total = jnp.sum(
        jnp.where(live0, low - in3[2], 0.0) + jnp.where(live1, high - in3[3], 0.0),
        axis=1, keepdims=True,
    )
    counts = count.astype(jnp.float32)
    scores = jnp.where(lane == 0, policy_total / counts, ratio_total / counts)
    scores_out[...] = scores[:, 0:2]
    mine = in3[t // 2]
    mine = jnp.where(half == 1, pltpu.roll(mine, 120, 1), mine)
    mine = jnp.where(lane + 8 * t < count, mine, 0.0)
    policy_out[...] = mine[:, 0:8]

    for d in range(1, NT):
        rs_copy(d).wait_send()
        tgt_copy(d).wait_send()
    for d in range(1, NX):
        xa_copy(d).wait_send()
    for k in steps:
        for side, j in streams:
            if exists(k, side, j):
                z_copy(True, k, side, j).wait_send()
                z_copy(False, k, side, j).wait_send()
    for g in range(9):
        for way in range(2):
            x_copy(g, way, 0).wait_send()
            x_copy(g, way, 1).wait_send()
        twin_copy(g, c).wait_send()

    def head_sent(k, carry):
        pair_copy(k).wait_send()
        across_copy(k).wait_send()
        forward_copy(k).wait_send()
        return carry

    lax.fori_loop(0, PIECES, head_sent, 0)

    for d in range(1, NX * NC):
        e1_copy(d).wait_send()
    ring_loop(lambda d, e: e2_copy(d, e).wait_send())


def per_device(
    queries,
    response_kv,
    cache_kv,
    residual,
    out_proj,
    norm_gain,
    lm_head,
    targets,
    resp_lengths,
    cache_lengths,
    owner_slot,
    sink_count,
    window_size,
):
    dma = pltpu.SemaphoreType.DMA
    vmem = pl.BlockSpec(memory_space=pltpu.VMEM)
    hbm = pl.BlockSpec(memory_space=pltpu.HBM)
    semaphores = [13] + [NT] * 4 + [PIECES] * 6 + [NX] * 2 + [16] * 4 + [36] * 2
    semaphores += [9] * 2 + [8] * 2 + [NZ * NT] * 2
    bf16, f32, i32 = jnp.bfloat16, jnp.float32, jnp.int32
    return pl.pallas_call(
        fused,
        out_shape=(jax.ShapeDtypeStruct((1, 8), f32), jax.ShapeDtypeStruct((1, 2), f32)),
        in_specs=[hbm] * 13,
        out_specs=(vmem, vmem),
        scratch_shapes=[
            pltpu.VMEM((2, D), f32),
            pltpu.VMEM((RESP // NT, REQS), i32),
            pltpu.VMEM((1, REQS), i32),
            pltpu.VMEM((1, REQS), i32),
            pltpu.VMEM((1, 1), i32),
            pltpu.VMEM((1, 1), i32),
            pltpu.VMEM((1, 1), i32),
            pltpu.VMEM((2, 1, RESP, FEAT), bf16),
            pltpu.VMEM((2, 2, KEYS, HEAD), bf16),
            pltpu.VMEM((2, FEAT, D), bf16),
            pltpu.VMEM((SLOTS, D), bf16),
            pltpu.VMEM((2, RESP, FEAT), bf16),
            pltpu.VMEM((2, RESP, D), f32),
            pltpu.VMEM((VOCAB_BLOCK, D), bf16),
            pltpu.VMEM((NX, 2 * CHUNKS, NC, SLOTS, D), bf16),
            pltpu.VMEM((NT, SLOTS, D), f32),
            pltpu.VMEM((NT, NZ, ROWS), i32),
            pltpu.VMEM((NZ, ROWS), i32),
            pltpu.VMEM((NZ, ROWS), i32),
            pltpu.VMEM((CHUNKS, 1, ROWS), i32),
            pltpu.VMEM((CHUNKS, REQS, ROWS), bf16),
            pltpu.VMEM((CHUNKS, 1, ROWS), f32),
            pltpu.VMEM((CHUNKS, 1, ROWS), f32),
            pltpu.VMEM((CHUNKS, 1, ROWS), f32),
            pltpu.VMEM((REQS, 128), f32),
            pltpu.VMEM((NX * NC, NZ, 128), f32),
            pltpu.VMEM((NZ, 1, 128), f32),
            pltpu.VMEM((NT, NZ, 1, 128), f32),
            pltpu.VMEM((NT, 1, 128), f32),
        ]
        + [dma((n,)) for n in semaphores],
        compiler_params=pltpu.CompilerParams(
            collective_id=0, has_side_effects=True, vmem_limit_bytes=63 << 20
        ),
    )(
        queries,
        response_kv.reshape(2, 2, RESP, KV_HEADS * HEAD),
        cache_kv.reshape(2, 2, CACHE, KV_HEADS * HEAD),
        residual.reshape(2, RESP, D),
        out_proj,
        norm_gain,
        lm_head,
        targets.T,
        resp_lengths.reshape(1, REQS),
        owner_slot.reshape(1, REQS),
        cache_lengths.reshape(1, 1),
        sink_count.reshape(1, 1),
        window_size.reshape(1, 1),
    )


def solution(mesh):
    in_specs = (
        P(None, "req", None, "tp"),
        P(None, "req", None, None, None),
        P(None, "req", None, None, None),
        P(None, "req", None, None),
        P(None, "tp", None),
        P(),
        P(None, "req", "tp"),
        P(None, "tp"),
        P(),
        P("req"),
        P(),
        P(),
        P(),
    )
    out_specs = (P("req", "tp"), P("req", None))
    return jax.shard_map(
        per_device, mesh=mesh, in_specs=in_specs, out_specs=out_specs, check_vma=False
    )
```

time: 111 us -> 104 us (0.937)
  local copies, waits for them, and re-layouts: 10.6 us -> 2.32 us
  Pallas kernels: 97.2 us -> 98.6 us
    unnamed x21 -> x2, local copies, waits for them, and re-layouts: 10.6 us -> 2.32 us
    pallas_call x1, Pallas kernels: 97.2 us -> 98.6 us  [per_device(): pl.pallas_call(fused, out_shape=(jax.ShapeDtypeStruct((1, 8), f32), jax.S...]
where the time goes in v3:
time: 104 us; the launch traced here: 103 us
  Pallas kernels  98.6 us (95%)
  between operations  2.58 us (2%)
  local copies, waits for them, and re-layouts  2.32 us (2%)
    pallas_call x1, Pallas kernels, per_device(): pl.pallas_call(fused, out_shape=(jax.ShapeDtypeStruct((1, 8), f32), jax.S...  98.6 us
    unnamed x2, local copies, waits for them, and re-layouts  2.32 us

profile of v3, /device:TPU:1, one launch (start us, length us, event | category | flops | bytes accessed | tf_op | source)
XLA Modules:
  0.0 103.5 jit_solution(13927771146448343209)
XLA Ops:
  2.6 98.6 %shard_map.140 = (f32[1,8]{1,0:T(1,128)}, f32[1,2]{1,0:T(1,128)}) custom-call(bf16[2,1,32,384]{3,2,1,0:T(8,128)(2,1)} %queries.1, bf16[2,2,32,256]{3,2,1,0:T(8,128)(2,1)} %bitcast.14, bf16[2,2,384,256]{3,2,1,0:T(8,128)(2,1)} %bitcast.12, bf16[2,32,1536]{2,1,0:T(8,128)(2,1)} %bitcast.13, bf16[2,384,1536]{2,1,0:T(8,128)(2,1)} %out_proj.1, f32[2,1536]{1,0:T(2,128)} %gain_in.1, ...), custom_call_target="tpu_custom_call" | custom-call | tf_op jit(solution)/shard_map/pallas_call | solution.py:578
  101.2 1.1 %copy.20 = f32[1,8]{1,0:T(1,128)} copy(f32[1,8]{1,0:T(1,128)} %get-tuple-element.4) | data formatting | bytes 64
  102.3 1.2 %copy.21 = f32[1,2]{1,0:T(1,128)} copy(f32[1,2]{1,0:T(1,128)} %get-tuple-element.5) | data formatting | bytes 16

commit v4 on v3

--- a/solution.py
+++ b/solution.py
@@ -21,13 +21,11 @@
 VOCAB_BLOCK = 1024
 PIECES = 4
 PIECE = VOCAB_BLOCK // PIECES
-CHUNKS = 8
-ROWS = 2 * NX * NC * SLOTS
-SPLIT = 128
-MIDDLE = SPLIT + 768
-A = pl.ds(0, SPLIT)
-B = pl.ds(SPLIT, D - SPLIT)
-B_PARTS = (pl.ds(SPLIT, MIDDLE - SPLIT), pl.ds(MIDDLE, D - MIDDLE))
+CHUNKS = 4
+ROWS = 4 * NX * NC * SLOTS
+BLOCK = 512
+FEATURE_HALVES = (pl.ds(0, D // 2), pl.ds(D // 2, D // 2))
+ALL = pl.ds(0, D)
 OWN = 4 * 4 - 1
 MESH = pl.DeviceIdType.MESH
 EXACT = lax.Precision.HIGHEST
@@ -52,7 +50,7 @@
     hbuf, rows, rs_in, tgt_in, tgt_all, own_all, wanted_buf, select_buf,
     peak_buf, norm_buf, pick_buf, outbuf, in1, ex2, in2, in3,
     load_sem, rs_s, rs_r, tg_s, tg_r, hp_s, hp_r, hq_s, hq_r, hf_s, hf_r,
-    xa_s, xa_r, za_s, za_r, zb_s, zb_r, xb_s, xb_r, c_s, c_r, e1_s, e1_r, e2_s, e2_r,
+    z_s, z_r, x_s, x_r, c_s, c_r, e1_s, e1_r, e2_s, e2_r,
 ):
     req = lax.axis_index("req")
     t = lax.axis_index("tp")
@@ -125,7 +123,7 @@
 
     req_sub = iota((REQS, ROWS), 0)
     row_lane = iota((REQS, ROWS), 1)
-    same_xc = ((req_sub >> 5) == (row_lane >> 6)) & ((req_sub & 1) == ((row_lane >> 4) & 1))
+    same_xc = ((req_sub >> 5) == (row_lane >> 7)) & ((req_sub & 1) == ((row_lane >> 4) & 1))
     same_z = ((iota((NZ, REQS), 1) >> 1) & (NZ - 1)) == iota((NZ, REQS), 0)
     zmask = jnp.where(same_z, 1.0, 0.0)
 
@@ -203,13 +201,18 @@
     for d in range(1, NT):
         rs_copy(d).start()
 
-    same_xc_wide = jnp.where(same_xc, 1.0, 0.0)
+    lane128 = iota((REQS, 128), 1)
+    sub128 = iota((REQS, 128), 0)
+    same_xc_lane = ((sub128 >> 5) == (lane128 >> 5)) & ((sub128 & 1) == ((lane128 >> 4) & 1))
     wide = jnp.concatenate(
         [zmask * targets[s : s + 1, :].astype(jnp.float32) for s in range(8)], axis=0
     )
-    wide = jnp.dot(wide, same_xc_wide, precision=EXACT, preferred_element_type=jnp.float32)
-    slot_lane = iota((NZ, ROWS), 1) & (SLOTS - 1)
-    placed = jnp.zeros((NZ, ROWS), jnp.float32)
+    wide = jnp.dot(
+        wide, jnp.where(same_xc_lane, 1.0, 0.0), precision=EXACT,
+        preferred_element_type=jnp.float32,
+    )
+    slot_lane = iota((NZ, 128), 1) & (SLOTS - 1)
+    placed = jnp.zeros((NZ, 128), jnp.float32)
     for s in range(8):
         placed = jnp.where(slot_lane == s + 8 * half, wide[NZ * s : NZ * s + NZ], placed)
     tgt_in[0] = placed.astype(jnp.int32)
@@ -220,16 +223,17 @@
     for d in range(1, NT):
         tgt_copy(d).start()
     own_all[...] = jnp.dot(
-        zmask * owner[...].astype(jnp.float32), same_xc_wide, precision=EXACT,
+        zmask * owner[...].astype(jnp.float32), jnp.where(same_xc, 1.0, 0.0), precision=EXACT,
         preferred_element_type=jnp.float32,
     ).astype(jnp.int32)
 
     def forward_head(k):
         across_recv(k).wait_recv()
         forward_copy(k).start()
-        if k + 1 < PIECES:
+        if k in (1, 2):
             pair_copy(k + 1).start()
 
+    pair_copy(1).start()
     across_copy(2).start()
     forward_head(0)
     across_copy(3).start()
@@ -258,28 +262,14 @@
 
     targets_of = [[away(side, 1), away(side, 2)] for side in range(2)]
 
-    def z_copy(part_a, k, side, j):
+    def z_copy(k, side, j):
         src = OWN if k == 1 else slot_of(k - 1, side, j)
         dst = slot_of(k, side, j)
         to = targets_of[side][j if k == 1 else 1]
-        if part_a:
-            return send(
-                rows.at[:, src, c, :, A], rows.at[:, dst, c, :, A], za_s.at[dst], za_r.at[dst], to, t
-            )
-        return send(
-            rows.at[x, src, c, :, B], rows.at[x, dst, c, :, B], zb_s.at[dst], zb_r.at[dst], to, t
-        )
+        return send(rows.at[x, src, c], rows.at[x, dst, c], z_s.at[dst], z_r.at[dst], to, t)
 
     beside = [index_of((x + d) % NX, z, c) for d in range(NX)]
     twin = index_of(x, z, 1 - c)
-
-    def xa_copy(d):
-        part = rows.at[x, OWN, c, :, A]
-        return send(part, part, xa_s.at[d], xa_r.at[d], beside[d], t)
-
-    def xa_recv(d):
-        part = rows.at[(x + NX - d) % NX, OWN, c, :, A]
-        return send(part, part, xa_s.at[d], xa_r.at[d], beside[d], t)
 
     groups = [(OWN, 1)] + [(4 * (k - 1) + 2 * side, 2) for k in steps for side in range(2)]
     groups[8] = (OWN - 1, 1)
@@ -291,9 +281,9 @@
     def x_copy(g, way, second, receiving=False):
         back = NX - 1 if way == 0 else 1
         block = (back if second else 0) + (back if receiving else 0)
-        part = x_part(g, block, B_PARTS[way] if second else B)
+        part = x_part(g, block, FEATURE_HALVES[way] if second else ALL)
         n = 4 * g + 2 * second + way
-        return send(part, part, xb_s.at[n], xb_r.at[n], beside[1 if way == 0 else NX - 1], t)
+        return send(part, part, x_s.at[n], x_r.at[n], beside[1 if way == 0 else NX - 1], t)
 
     def twin_copy(g, core):
         start, size = groups[g]
@@ -323,48 +313,49 @@
             for j in range(2):
                 if not exists(k, side, j):
                     continue
-                for part_a in (True, False):
-                    z_copy(part_a, k, side, j).wait_recv()
-                    if k < 4 and exists(k + 1, side, j):
-                        z_copy(part_a, k + 1, side, j).start()
+                z_copy(k, side, j).wait_recv()
+                if k < 4 and exists(k + 1, side, j):
+                    z_copy(k + 1, side, j).start()
             x_send(2 * k - 1 + side)
 
-    for d in range(1, NX):
-        xa_copy(d).start()
     for j in range(2):
         for side in range(2):
-            z_copy(False, 1, side, j).start()
+            z_copy(1, side, j).start()
     x_send(0)
-    for d in range(1, NX):
-        xa_recv(d).wait_recv()
-    for j in range(2):
-        for side in range(2):
-            z_copy(True, 1, side, j).start()
     forward_head(1)
 
-    tgt_own = jnp.zeros((NZ, ROWS), jnp.int32)
+    tgt_own = jnp.zeros((NZ, 128), jnp.int32)
     for d in range(NT):
         if d:
             tgt_copy(d).wait_recv()
         wanted_half = ((t + NT - d) % NT) // 2 == half
         tgt_own = tgt_own + jnp.where(wanted_half, tgt_in[d], 0)
-    tgt_all[...] = tgt_own - req * VOCAB_BLOCK
+    small_lane = ((iota((128, ROWS), 1) >> 7) << 5) + (iota((128, ROWS), 1) & 31)
+    repeat = jnp.where(small_lane == iota((128, ROWS), 0), 1.0, 0.0)
+    tgt_wide = jnp.dot(
+        tgt_own.astype(jnp.float32), repeat, precision=EXACT, preferred_element_type=jnp.float32
+    )
+    tgt_all[...] = tgt_wide.astype(jnp.int32) - req * VOCAB_BLOCK
     outbuf[...] = jnp.zeros_like(outbuf)
     peak_buf[...] = jnp.full_like(peak_buf, -jnp.inf)
     norm_buf[...] = jnp.zeros_like(norm_buf)
     pick_buf[...] = jnp.zeros_like(pick_buf)
 
-    def prepare(n):
-        if n % 2 == 0:
-            z1, z2 = (z + NZ - n - 1) % NZ, (z + NZ - n - 2) % NZ
-        else:
-            z1, z2 = (z + n) % NZ, (z + (n + 1) % 8) % NZ
-        first = (iota((1, ROWS), 1) & 32) == 0
-        wanted_buf[n] = jnp.where(first, tgt_all[pl.ds(z1, 1), :], tgt_all[pl.ds(z2, 1), :])
+    def prepare(k):
+        near, far = 2 * k + 1, 2 * k + 2
+        places = [(z + NZ - near) % NZ, (z + NZ - far) % NZ, (z + near) % NZ, (z + far % 8) % NZ]
+        place = (iota((1, ROWS), 1) >> 5) & 3
+
+        def pick(table):
+            found = table[pl.ds(places[3], 1), :]
+            for i in range(3):
+                found = jnp.where(place == i, table[pl.ds(places[i], 1), :], found)
+            return found
+
+        wanted_buf[k] = pick(tgt_all)
         sub = iota((REQS, ROWS), 0)
         dest = ((sub >> 5) * NZ + (sub & (NZ - 1))) * NC + ((sub >> 4) & 1)
-        place = jnp.where(first, own_all[pl.ds(z1, 1), :], own_all[pl.ds(z2, 1), :])
-        select_buf[n] = jnp.where(dest == place, 1.0, 0.0).astype(jnp.bfloat16)
+        select_buf[k] = jnp.where(dest == pick(own_all), 1.0, 0.0).astype(jnp.bfloat16)
 
     def head_ready(k):
         pair_recv(k).wait_recv()
@@ -374,11 +365,11 @@
         def unit(i, carry):
             k = k0 + i // (p1 - p0)
             p = p0 + i % (p1 - p0)
-            base = pl.multiple_of(p * PIECE, PIECE)
-            chunk = rows[:, pl.ds(2 * k, 2)].reshape(ROWS, D)
-            logits = nt_dot(hbuf[pl.ds(base, PIECE), :], chunk)
+            base = pl.multiple_of(p * BLOCK, BLOCK)
+            chunk = rows[:, pl.ds(4 * k, 4)].reshape(ROWS, D)
+            logits = nt_dot(hbuf[pl.ds(base, BLOCK), :], chunk)
             peak = jnp.max(logits, axis=0, keepdims=True)
-            hit = iota((PIECE, ROWS), 0) == wanted_buf[k] - base
+            hit = iota((BLOCK, ROWS), 0) == wanted_buf[k] - base
             pick_buf[k] += jnp.sum(jnp.where(hit, logits, 0.0), axis=0, keepdims=True)
             old = peak_buf[k]
             new = jnp.maximum(old, peak)
@@ -392,8 +383,8 @@
     x_pass(0)
     arrive(1)
     forward_head(2)
-    for n in range(4):
-        prepare(n)
+    prepare(0)
+    prepare(1)
     x_done(0)
 
     x_pass(1)
@@ -402,8 +393,8 @@
     forward_head(3)
     x_done(1)
     x_done(2)
-    for n in range(4, CHUNKS):
-        prepare(n)
+    prepare(2)
+    prepare(3)
 
     x_pass(3)
     x_pass(4)
@@ -414,7 +405,7 @@
     head_ready(0)
     head_ready(1)
     other_core(1, 2)
-    units(0, 2, 0, 2)
+    units(0, 1, 0, 1)
 
     x_pass(5)
     x_pass(6)
@@ -422,20 +413,19 @@
     x_done(5)
     x_done(6)
     other_core(3, 4)
-    units(2, 4, 0, 2)
+    units(1, 2, 0, 1)
     x_pass(7)
     x_pass(8)
+    other_core(5, 6)
+    units(2, 3, 0, 1)
     head_ready(2)
-    units(0, 4, 2, 3)
     head_ready(3)
-    units(0, 4, 3, 4)
-    other_core(5, 6)
-    units(4, 6, 0, 2)
+    units(0, 2, 1, 2)
     x_done(7)
     x_done(8)
-    units(4, 6, 2, 4)
+    units(2, 3, 1, 2)
     other_core(7, 8, 0)
-    units(6, 8, 0, 4)
+    units(3, 4, 0, 2)
 
     def finish(k, carry):
         sub = iota((2 * SLOTS, ROWS), 0)
@@ -528,13 +518,10 @@
     for d in range(1, NT):
         rs_copy(d).wait_send()
         tgt_copy(d).wait_send()
-    for d in range(1, NX):
-        xa_copy(d).wait_send()
     for k in steps:
         for side, j in streams:
             if exists(k, side, j):
-                z_copy(True, k, side, j).wait_send()
-                z_copy(False, k, side, j).wait_send()
+                z_copy(k, side, j).wait_send()
     for g in range(9):
         for way in range(2):
             x_copy(g, way, 0).wait_send()
@@ -572,7 +559,7 @@
     dma = pltpu.SemaphoreType.DMA
     vmem = pl.BlockSpec(memory_space=pltpu.VMEM)
     hbm = pl.BlockSpec(memory_space=pltpu.HBM)
-    semaphores = [13] + [NT] * 4 + [PIECES] * 6 + [NX] * 2 + [16] * 4 + [36] * 2
+    semaphores = [13] + [NT] * 4 + [PIECES] * 6 + [16] * 2 + [36] * 2
     semaphores += [9] * 2 + [8] * 2 + [NZ * NT] * 2
     bf16, f32, i32 = jnp.bfloat16, jnp.float32, jnp.int32
     return pl.pallas_call(
@@ -595,9 +582,9 @@
             pltpu.VMEM((2, RESP, FEAT), bf16),
             pltpu.VMEM((2, RESP, D), f32),
             pltpu.VMEM((VOCAB_BLOCK, D), bf16),
-            pltpu.VMEM((NX, 2 * CHUNKS, NC, SLOTS, D), bf16),
+            pltpu.VMEM((NX, NZ, NC, SLOTS, D), bf16),
             pltpu.VMEM((NT, SLOTS, D), f32),
-            pltpu.VMEM((NT, NZ, ROWS), i32),
+            pltpu.VMEM((NT, NZ, 128), i32),
             pltpu.VMEM((NZ, ROWS), i32),
             pltpu.VMEM((NZ, ROWS), i32),
             pltpu.VMEM((CHUNKS, 1, ROWS), i32),

time: 104 us -> 97.7 us (0.939)
  Pallas kernels: 98.6 us -> 92.6 us
    pallas_call x1, Pallas kernels: 98.6 us -> 92.6 us  [per_device(): pl.pallas_call(fused, out_shape=(jax.ShapeDtypeStruct((1, 8), f32), jax.S...]
where the time goes in v4:
time: 97.7 us; the launch traced here: 97.5 us
  Pallas kernels  92.6 us (95%)
  between operations  2.58 us (3%)
  local copies, waits for them, and re-layouts  2.32 us (2%)
    pallas_call x1, Pallas kernels, per_device(): pl.pallas_call(fused, out_shape=(jax.ShapeDtypeStruct((1, 8), f32), jax.S...  92.6 us
    unnamed x2, local copies, waits for them, and re-layouts  2.32 us

profile of v4, /device:TPU:1, one launch (start us, length us, event | category | flops | bytes accessed | tf_op | source)
XLA Modules:
  0.0 97.5 jit_solution(9323244809391221636)
XLA Ops:
  2.6 92.6 %shard_map.140 = (f32[1,8]{1,0:T(1,128)}, f32[1,2]{1,0:T(1,128)}) custom-call(bf16[2,1,32,384]{3,2,1,0:T(8,128)(2,1)} %queries.1, bf16[2,2,32,256]{3,2,1,0:T(8,128)(2,1)} %bitcast.14, bf16[2,2,384,256]{3,2,1,0:T(8,128)(2,1)} %bitcast.12, bf16[2,32,1536]{2,1,0:T(8,128)(2,1)} %bitcast.13, bf16[2,384,1536]{2,1,0:T(8,128)(2,1)} %out_proj.1, f32[2,1536]{1,0:T(2,128)} %gain_in.1, ...), custom_call_target="tpu_custom_call" | custom-call | tf_op jit(solution)/shard_map/pallas_call | solution.py:565
  95.2 1.1 %copy.20 = f32[1,8]{1,0:T(1,128)} copy(f32[1,8]{1,0:T(1,128)} %get-tuple-element.4) | data formatting | bytes 64
  96.3 1.2 %copy.21 = f32[1,2]{1,0:T(1,128)} copy(f32[1,2]{1,0:T(1,128)} %get-tuple-element.5) | data formatting | bytes 16

commit v5 on v4

--- a/solution.py
+++ b/solution.py
@@ -127,8 +127,6 @@
     same_z = ((iota((NZ, REQS), 1) >> 1) & (NZ - 1)) == iota((NZ, REQS), 0)
     zmask = jnp.where(same_z, 1.0, 0.0)
 
-    pl.semaphore_wait(barrier, (NX * NC - 1) + (NT * NZ - 1))
-
     def piece(k):
         return pl.ds(k * PIECE, PIECE)
 
@@ -160,10 +158,6 @@
     def forward_recv(k):
         part = hbuf.at[piece(k), lanes(NT - 1 - pair)]
         return send(part, part, hf_s.at[k], hf_r.at[k], req, pair)
-
-    across_copy(0).start()
-    pair_copy(0).start()
-    across_copy(1).start()
 
     for copy in small + loads[:3]:
         copy.wait()
@@ -191,6 +185,8 @@
     for m in range(2):
         partial[m] = jnp.dot(attbuf[m], wbuf[m], preferred_element_type=jnp.float32)
 
+    pl.semaphore_wait(barrier, (NX * NC - 1) + (NT * NZ - 1))
+
     def rs_copy(d):
         pt = (t + d) % NT
         start = pl.multiple_of((pt % 2) * SLOTS, SLOTS)
@@ -200,6 +196,10 @@
 
     for d in range(1, NT):
         rs_copy(d).start()
+    for k in range(PIECES):
+        if k < 2:
+            pair_copy(k).start()
+        across_copy(k).start()
 
     lane128 = iota((REQS, 128), 1)
     sub128 = iota((REQS, 128), 0)
@@ -230,13 +230,8 @@
     def forward_head(k):
         across_recv(k).wait_recv()
         forward_copy(k).start()
-        if k in (1, 2):
-            pair_copy(k + 1).start()
-
-    pair_copy(1).start()
-    across_copy(2).start()
-    forward_head(0)
-    across_copy(3).start()
+        if k < 2:
+            pair_copy(k + 2).start()
 
     loads[4].wait()
     hidden = resbuf[...].astype(jnp.float32)
@@ -322,7 +317,7 @@
         for side in range(2):
             z_copy(1, side, j).start()
     x_send(0)
-    forward_head(1)
+    forward_head(0)
 
     tgt_own = jnp.zeros((NZ, 128), jnp.int32)
     for d in range(NT):
@@ -380,25 +375,30 @@
 
         lax.fori_loop(0, (k1 - k0) * (p1 - p0), unit, 0)
 
+    arrive(1)
     x_pass(0)
-    arrive(1)
-    forward_head(2)
+    forward_head(1)
     prepare(0)
     prepare(1)
-    x_done(0)
-
+
+    arrive(2)
     x_pass(1)
     x_pass(2)
-    arrive(2)
+    forward_head(2)
+    x_done(0)
+    prepare(2)
+    prepare(3)
+
+    arrive(3)
+    x_pass(3)
+    x_pass(4)
     forward_head(3)
     x_done(1)
     x_done(2)
-    prepare(2)
-    prepare(3)
-
-    x_pass(3)
-    x_pass(4)
-    arrive(3)
+
+    arrive(4)
+    x_pass(5)
+    x_pass(6)
     x_done(3)
     x_done(4)
     own_head.wait()
@@ -406,24 +406,19 @@
     head_ready(1)
     other_core(1, 2)
     units(0, 1, 0, 1)
-
-    x_pass(5)
-    x_pass(6)
-    arrive(4)
+    x_pass(7)
+    x_pass(8)
     x_done(5)
     x_done(6)
     other_core(3, 4)
     units(1, 2, 0, 1)
-    x_pass(7)
-    x_pass(8)
     other_core(5, 6)
     units(2, 3, 0, 1)
+    x_done(7)
+    x_done(8)
     head_ready(2)
     head_ready(3)
-    units(0, 2, 1, 2)
-    x_done(7)
-    x_done(8)
-    units(2, 3, 1, 2)
+    units(0, 3, 1, 2)
     other_core(7, 8, 0)
     units(3, 4, 0, 2)
 

time: 97.7 us -> 100 us (1.024)
  Pallas kernels: 92.6 us -> 95 us
    pallas_call x1, Pallas kernels: 92.6 us -> 95 us  [per_device(): pl.pallas_call(fused, out_shape=(jax.ShapeDtypeStruct((1, 8), f32), jax.S...]
where the time goes in v5:
time: 100 us; the launch traced here: 99.9 us
  Pallas kernels  95 us (95%)
  between operations  2.58 us (3%)
  local copies, waits for them, and re-layouts  2.32 us (2%)
    pallas_call x1, Pallas kernels, per_device(): pl.pallas_call(fused, out_shape=(jax.ShapeDtypeStruct((1, 8), f32), jax.S...  95 us
    unnamed x2, local copies, waits for them, and re-layouts  2.32 us

profile of v5, /device:TPU:1, one launch (start us, length us, event | category | flops | bytes accessed | tf_op | source)
XLA Modules:
  0.0 99.9 jit_solution(9350083564343092811)
XLA Ops:
  2.6 95.0 %shard_map.140 = (f32[1,8]{1,0:T(1,128)}, f32[1,2]{1,0:T(1,128)}) custom-call(bf16[2,1,32,384]{3,2,1,0:T(8,128)(2,1)} %queries.1, bf16[2,2,32,256]{3,2,1,0:T(8,128)(2,1)} %bitcast.14, bf16[2,2,384,256]{3,2,1,0:T(8,128)(2,1)} %bitcast.12, bf16[2,32,1536]{2,1,0:T(8,128)(2,1)} %bitcast.13, bf16[2,384,1536]{2,1,0:T(8,128)(2,1)} %out_proj.1, f32[2,1536]{1,0:T(2,128)} %gain_in.1, ...), custom_call_target="tpu_custom_call" | custom-call | tf_op jit(solution)/shard_map/pallas_call | solution.py:560
  97.5 1.1 %copy.20 = f32[1,8]{1,0:T(1,128)} copy(f32[1,8]{1,0:T(1,128)} %get-tuple-element.4) | data formatting | bytes 64
  98.7 1.2 %copy.21 = f32[1,2]{1,0:T(1,128)} copy(f32[1,2]{1,0:T(1,128)} %get-tuple-element.5) | data formatting | bytes 16

commit v6 on v4

--- a/solution.py
+++ b/solution.py
@@ -380,50 +380,49 @@
 
         lax.fori_loop(0, (k1 - k0) * (p1 - p0), unit, 0)
 
+    arrive(1)
     x_pass(0)
-    arrive(1)
     forward_head(2)
     prepare(0)
     prepare(1)
-    x_done(0)
-
+
+    arrive(2)
     x_pass(1)
     x_pass(2)
-    arrive(2)
+    x_done(0)
     forward_head(3)
+    prepare(2)
+    prepare(3)
+
+    arrive(3)
+    x_pass(3)
+    x_pass(4)
     x_done(1)
     x_done(2)
-    prepare(2)
-    prepare(3)
-
-    x_pass(3)
-    x_pass(4)
-    arrive(3)
-    x_done(3)
-    x_done(4)
     own_head.wait()
     head_ready(0)
     head_ready(1)
+
+    arrive(4)
+    x_pass(5)
+    x_pass(6)
+    x_done(3)
+    x_done(4)
     other_core(1, 2)
     units(0, 1, 0, 1)
-
-    x_pass(5)
-    x_pass(6)
-    arrive(4)
+    x_pass(7)
+    x_pass(8)
     x_done(5)
     x_done(6)
     other_core(3, 4)
     units(1, 2, 0, 1)
-    x_pass(7)
-    x_pass(8)
+    x_done(7)
+    x_done(8)
     other_core(5, 6)
     units(2, 3, 0, 1)
     head_ready(2)
     head_ready(3)
-    units(0, 2, 1, 2)
-    x_done(7)
-    x_done(8)
-    units(2, 3, 1, 2)
+    units(0, 3, 1, 2)
     other_core(7, 8, 0)
     units(3, 4, 0, 2)
 

time: 97.7 us -> 95.8 us (0.981)
  Pallas kernels: 92.6 us -> 90.7 us
    pallas_call x1, Pallas kernels: 92.6 us -> 90.7 us  [per_device(): pl.pallas_call(fused, out_shape=(jax.ShapeDtypeStruct((1, 8), f32), jax.S...]
where the time goes in v6:
time: 95.8 us; the launch traced here: 95.6 us
  Pallas kernels  90.7 us (95%)
  between operations  2.58 us (3%)
  local copies, waits for them, and re-layouts  2.32 us (2%)
    pallas_call x1, Pallas kernels, per_device(): pl.pallas_call(fused, out_shape=(jax.ShapeDtypeStruct((1, 8), f32), jax.S...  90.7 us
    unnamed x2, local copies, waits for them, and re-layouts  2.32 us

profile of v6, /device:TPU:1, one launch (start us, length us, event | category | flops | bytes accessed | tf_op | source)
XLA Modules:
  0.0 95.6 jit_solution(315501704116403510)
XLA Ops:
  2.6 90.7 %shard_map.140 = (f32[1,8]{1,0:T(1,128)}, f32[1,2]{1,0:T(1,128)}) custom-call(bf16[2,1,32,384]{3,2,1,0:T(8,128)(2,1)} %queries.1, bf16[2,2,32,256]{3,2,1,0:T(8,128)(2,1)} %bitcast.14, bf16[2,2,384,256]{3,2,1,0:T(8,128)(2,1)} %bitcast.12, bf16[2,32,1536]{2,1,0:T(8,128)(2,1)} %bitcast.13, bf16[2,384,1536]{2,1,0:T(8,128)(2,1)} %out_proj.1, f32[2,1536]{1,0:T(2,128)} %gain_in.1, ...), custom_call_target="tpu_custom_call" | custom-call | tf_op jit(solution)/shard_map/pallas_call | solution.py:564
  93.3 1.1 %copy.20 = f32[1,8]{1,0:T(1,128)} copy(f32[1,8]{1,0:T(1,128)} %get-tuple-element.4) | data formatting | bytes 64
  94.5 1.2 %copy.21 = f32[1,2]{1,0:T(1,128)} copy(f32[1,2]{1,0:T(1,128)} %get-tuple-element.5) | data formatting | bytes 16

commit v7 on v6

--- a/solution.py
+++ b/solution.py
@@ -72,9 +72,6 @@
             device_id={"req": preq, "tp": pt}, device_id_type=MESH,
         )
 
-    def lanes(source):
-        return pl.ds(pl.multiple_of(source * FEAT, FEAT), FEAT)
-
     barrier = pltpu.get_barrier_semaphore()
 
     def greet(preq, pt):
@@ -116,7 +113,7 @@
     small = [
         pltpu.make_async_copy(src, dst, load_sem.at[6 + i]) for i, (src, dst) in enumerate(small)
     ]
-    own_head = pltpu.make_async_copy(head.at[model], hbuf.at[:, lanes(t)], load_sem.at[5])
+    own_head = pltpu.make_async_copy(head.at[model], hbuf.at[t], load_sem.at[5])
     for copy in small + loads:
         copy.start()
     own_head.start()
@@ -134,31 +131,31 @@
 
     def pair_copy(k):
         return send(
-            head.at[model, piece(k)], hbuf.at[piece(k), lanes(t)], hp_s.at[k], hp_r.at[k], req, pair
+            head.at[model, piece(k)], hbuf.at[t, piece(k)], hp_s.at[k], hp_r.at[k], req, pair
         )
 
     def across_copy(k):
         return send(
-            head.at[1 - model, piece(k)], hbuf.at[piece(k), lanes(t)], hq_s.at[k], hq_r.at[k],
+            head.at[1 - model, piece(k)], hbuf.at[t, piece(k)], hq_s.at[k], hq_r.at[k],
             req, across,
         )
 
     def across_recv(k):
         return send(
-            head.at[1 - model, piece(k)], hbuf.at[piece(k), lanes(across)], hq_s.at[k], hq_r.at[k],
+            head.at[1 - model, piece(k)], hbuf.at[across, piece(k)], hq_s.at[k], hq_r.at[k],
             req, across,
         )
 
     def forward_copy(k):
-        part = hbuf.at[piece(k), lanes(across)]
+        part = hbuf.at[across, piece(k)]
         return send(part, part, hf_s.at[k], hf_r.at[k], req, pair)
 
     def pair_recv(k):
-        part = hbuf.at[piece(k), lanes(pair)]
+        part = hbuf.at[pair, piece(k)]
         return send(part, part, hp_s.at[k], hp_r.at[k], req, pair)
 
     def forward_recv(k):
-        part = hbuf.at[piece(k), lanes(NT - 1 - pair)]
+        part = hbuf.at[NT - 1 - pair, piece(k)]
         return send(part, part, hf_s.at[k], hf_r.at[k], req, pair)
 
     across_copy(0).start()
@@ -367,7 +364,8 @@
             p = p0 + i % (p1 - p0)
             base = pl.multiple_of(p * BLOCK, BLOCK)
             chunk = rows[:, pl.ds(4 * k, 4)].reshape(ROWS, D)
-            logits = nt_dot(hbuf[pl.ds(base, BLOCK), :], chunk)
+            block = [hbuf[q, pl.ds(base, BLOCK), :] for q in range(NT)]
+            logits = nt_dot(jnp.concatenate(block, axis=1), chunk)
             peak = jnp.max(logits, axis=0, keepdims=True)
             hit = iota((BLOCK, ROWS), 0) == wanted_buf[k] - base
             pick_buf[k] += jnp.sum(jnp.where(hit, logits, 0.0), axis=0, keepdims=True)
@@ -423,9 +421,6 @@
     head_ready(2)
     head_ready(3)
     units(0, 3, 1, 2)
-    other_core(7, 8, 0)
-    units(3, 4, 0, 2)
-
     def finish(k, carry):
         sub = iota((2 * SLOTS, ROWS), 0)
         slot = iota((2 * SLOTS, ROWS), 1) & (SLOTS - 1)
@@ -439,7 +434,10 @@
         outbuf[...] += nt_dot(select_buf[k], jnp.concatenate(terms, axis=0))
         return carry
 
-    lax.fori_loop(0, CHUNKS, finish, 0)
+    lax.fori_loop(0, 3, finish, 0)
+    other_core(7, 8, 0)
+    units(3, 4, 0, 2)
+    finish(3, 0)
     found = outbuf[...]
     outbuf[...] = (found + pltpu.roll(found, 96, 1)) + pltpu.roll(found, 64, 1)
 
@@ -580,7 +578,7 @@
             pltpu.VMEM((SLOTS, D), bf16),
             pltpu.VMEM((2, RESP, FEAT), bf16),
             pltpu.VMEM((2, RESP, D), f32),
-            pltpu.VMEM((VOCAB_BLOCK, D), bf16),
+            pltpu.VMEM((NT, VOCAB_BLOCK, FEAT), bf16),
             pltpu.VMEM((NX, NZ, NC, SLOTS, D), bf16),
             pltpu.VMEM((NT, SLOTS, D), f32),
             pltpu.VMEM((NT, NZ, 128), i32),

time: 95.8 us -> 95.8 us (level)
  no operation moved by 1% of the time
where the time goes in v7:
time: 95.8 us; the launch traced here: 95.6 us
  Pallas kernels  90.7 us (95%)
  between operations  2.58 us (3%)
  local copies, waits for them, and re-layouts  2.32 us (2%)
    pallas_call x1, Pallas kernels, per_device(): pl.pallas_call(fused, out_shape=(jax.ShapeDtypeStruct((1, 8), f32), jax.S...  90.7 us
    unnamed x2, local copies, waits for them, and re-layouts  2.32 us

profile of v7, /device:TPU:1, one launch (start us, length us, event | category | flops | bytes accessed | tf_op | source)
XLA Modules:
  0.0 95.6 jit_solution(9813079309883138333)
XLA Ops:
  2.6 90.7 %shard_map.140 = (f32[1,8]{1,0:T(1,128)}, f32[1,2]{1,0:T(1,128)}) custom-call(bf16[2,1,32,384]{3,2,1,0:T(8,128)(2,1)} %queries.1, bf16[2,2,32,256]{3,2,1,0:T(8,128)(2,1)} %bitcast.14, bf16[2,2,384,256]{3,2,1,0:T(8,128)(2,1)} %bitcast.12, bf16[2,32,1536]{2,1,0:T(8,128)(2,1)} %bitcast.13, bf16[2,384,1536]{2,1,0:T(8,128)(2,1)} %out_proj.1, f32[2,1536]{1,0:T(2,128)} %gain_in.1, ...), custom_call_target="tpu_custom_call" | custom-call | tf_op jit(solution)/shard_map/pallas_call | solution.py:562
  93.3 1.1 %copy.20 = f32[1,8]{1,0:T(1,128)} copy(f32[1,8]{1,0:T(1,128)} %get-tuple-element.4) | data formatting | bytes 64
  94.4 1.2 %copy.21 = f32[1,2]{1,0:T(1,128)} copy(f32[1,2]{1,0:T(1,128)} %get-tuple-element.5) | data formatting | bytes 16
